TPU v7x, 256 devices: a whole 4x4x8 slice. The times are simulated.
256 devices in a mesh: prompt: 16 (over z, core), comp: 16 (over x, y).
Axes of the slice: x: 4, y: 4, z: 8, core: 2. Of those that a mesh axis runs over, the one named last changes fastest.
Arguments:
- prompt_inner: bfloat16 [4096, 16384], P('prompt', 'comp'), may hold values from -0.59765625 to 0.59765625
- prompt_proj: bfloat16 [4096, 4096], P('prompt'), may hold values from -0.8984375 to 0.8984375
- prompt_step: float32 [256, 4096], P('comp', 'prompt')
- completion_inner: bfloat16 [32, 256, 16384], P('comp', None, 'prompt'), may hold values from -0.59765625 to 0.59765625
- completion_gate: bfloat16 [32, 256, 16384], P('comp', None, 'prompt'), may hold values from -12 to 12
- completion_projections: bfloat16 [32, 256, 4096], P('comp'), may hold values from -0.8984375 to 0.8984375
- sample_step: float32 [256, 32, 256], P('prompt', 'comp')
- sample_length: int32 [32], P('comp'), may hold values from 1 to 256, as said below
- decay_log: float32 [256], replicated
- conv_inner: bfloat16 [4, 16384], replicated, may hold values from -3 to 3
- conv_proj: bfloat16 [4, 4096], replicated, may hold values from -3 to 3
- norm_gain: float32 [16384], P('prompt'), may hold values from 0.5 to 1.5
Outputs:
- sample_out: bfloat16 [32, 256, 16384], P('comp', None, 'prompt')
Inputs may be any that keep to these rules, and one draw needn't show every extreme that they name: `sample_length`: some completion slot is full.
All inputs are finite; a program needn't handle non-finite values.
Results may differ from a plain program's by a relative error of at most 0.014.
Values may be sent and summed in bfloat16 or wider, within the bound.
A program may use at most 128 MiB of HBM per device.

v0:
```python
import jax
import jax.numpy as jnp
from jax import lax
from jax.sharding import PartitionSpec as P

STATE_HEADS = 256
HEAD_WIDTH = 64
STATE_WIDTH = 256
STATE_GROUPS = 8
CONV = 4
BLOCK = 128


EPS = 1e-05
HIGHEST = lax.Precision.HIGHEST


def from_behind(block, axis, distance):
    devices = range(lax.axis_size(axis))
    route = [(i - distance, i) for i in devices if i - distance in devices]
    return lax.ppermute(block, axis, route)


def carried_in(array, axis, combine, identity):
    peers, position = (lax.axis_size(axis), lax.axis_index(axis))
    everything = jax.tree.map(
        lambda part, kind: lax.all_gather(part.astype(kind), axis),
        array,
        (jnp.bfloat16, jnp.bfloat16),
    )
    start = jax.tree.map(
        lambda part, zero: jnp.broadcast_to(jnp.asarray(zero, part.dtype), part.shape),
        array,
        identity,
    )

    def hop(k, before):
        reached = k < position
        new = combine(
            before, jax.tree.map(lambda part, own: part[k].astype(own.dtype), everything, array)
        )
        return jax.tree.map(lambda a, b: jnp.where(reached, a, b), new, before)

    return lax.fori_loop(0, peers, hop, start)


def from_root(array, axis, root):
    mine = lax.axis_index(axis) == root
    return lax.psum(jnp.where(mine, array, jnp.zeros_like(array)), axis)


def from_partner(block, axis, stride):
    count = lax.axis_size(axis)
    route = []
    for low in range(count):
        high = low | 1 << stride
        if high != low and high < count:
            route += [(low, high), (high, low)]
    return lax.ppermute(block, axis, route)


def causal_conv(source, kernel, leading):
    padded = jnp.concatenate([leading, source], axis=0).astype(jnp.float32)
    kernel_wide = kernel.astype(jnp.float32)
    row_count = source.shape[0]
    summed = jnp.zeros(source.shape, jnp.float32)
    for offset in range(kernel.shape[0]):
        summed = summed + kernel_wide[offset] * padded[offset : offset + row_count]
    return jax.nn.silu(summed).astype(jnp.bfloat16)


def block_scan(state_in, inner_blk, b_blk, c_blk, step_blk, rate_vals):
    cumul = jnp.cumsum(-rate_vals[:, :, None] * step_blk, axis=2)
    scores = jnp.einsum("ign,jgn->gij", c_blk, b_blk, preferred_element_type=jnp.float32)
    spread_log = cumul[:, :, :, None] - cumul[:, :, None, :]
    length_q = step_blk.shape[2]
    causal = jnp.arange(length_q)[:, None] >= jnp.arange(length_q)[None, :]
    decay_mat = jnp.exp(jnp.where(causal, spread_log, -jnp.inf))
    mixer_w = (scores[:, None] * decay_mat * step_blk[:, :, None, :]).astype(jnp.bfloat16)
    intra_part = jnp.einsum(
        "gkij,jgkd->igkd", mixer_w, inner_blk, preferred_element_type=jnp.float32
    )
    readout = jnp.einsum("ign,gkdn->igkd", c_blk.astype(jnp.float32), state_in, precision=HIGHEST)
    inter_part = jnp.transpose(jnp.exp(cumul), (2, 0, 1))[..., None] * readout
    weights = jnp.exp(cumul[:, :, -1:] - cumul) * step_blk
    packed = (inner_blk.astype(jnp.float32) * jnp.transpose(weights, (2, 0, 1))[..., None]).astype(
        jnp.bfloat16
    )
    fresh_part = jnp.einsum("jgn,jgkd->gkdn", b_blk, packed, preferred_element_type=jnp.float32)
    return (
        intra_part + inter_part,
        jnp.exp(cumul[:, :, -1])[..., None, None] * state_in + fresh_part,
    )


def local(
    prompt_inner,
    prompt_proj,
    prompt_step,
    completion_inner,
    completion_gate,
    completion_projections,
    sample_step,
    sample_length,
    decay_log,
    conv_inner,
    conv_proj,
    norm_gain,
):
    prompt_count = lax.axis_size("prompt")
    prompt_idx = lax.axis_index("prompt")
    column_idx = lax.axis_index("comp")
    heads_group = STATE_HEADS // STATE_GROUPS
    heads_col = prompt_step.shape[0]
    heads_row = sample_step.shape[0]
    state_feats = STATE_GROUPS * STATE_WIDTH
    lag_rows = CONV - 1
    rows_prompt = prompt_inner.shape[0]
    prev_inner, prev_proj = from_behind(
        (
            prompt_inner[rows_prompt - lag_rows :],
            prompt_proj[rows_prompt - lag_rows :, :state_feats],
        ),
        "prompt",
        1,
    )
    col_start = column_idx * heads_col
    conv_col = lax.dynamic_slice_in_dim(
        conv_inner, col_start * HEAD_WIDTH, heads_col * HEAD_WIDTH, 1
    )
    inner_conv = causal_conv(prompt_inner, conv_col, prev_inner)
    b_conv = causal_conv(prompt_proj[:, :state_feats], conv_proj[:, :state_feats], prev_proj)
    rate_col = jnp.exp(lax.dynamic_slice_in_dim(decay_log, col_start, heads_col, 0))
    step_col = jax.nn.softplus(prompt_step)
    cumul = jnp.cumsum(-rate_col[:, None] * step_col, axis=1)
    local_log = cumul[:, -1]
    weight_col = jnp.exp(local_log[:, None] - cumul) * step_col
    group_span = max(1, heads_col // heads_group)
    per_group = heads_col // group_span
    group_start = col_start // heads_group
    b_select = lax.dynamic_slice_in_dim(
        b_conv.reshape(rows_prompt, STATE_GROUPS, STATE_WIDTH), group_start, group_span, 1
    ).astype(jnp.float32)
    scaled = (
        inner_conv.astype(jnp.float32).reshape(rows_prompt, heads_col, HEAD_WIDTH)
        * jnp.transpose(weight_col)[:, :, None]
    )
    scaled = scaled.reshape(rows_prompt, group_span, per_group, HEAD_WIDTH)
    local_state = jnp.einsum("tgn,tghd->ghdn", b_select, scaled, precision=HIGHEST).reshape(
        heads_col, HEAD_WIDTH, STATE_WIDTH
    )
    own_inner = prompt_inner[rows_prompt - lag_rows :].astype(jnp.float32)
    own_proj = prompt_proj[rows_prompt - lag_rows :].astype(jnp.float32)
    last_index = prompt_count - 1
    head_start = prompt_idx * heads_row
    owner = head_start // heads_col

    def combine(earlier, later):
        return (earlier[0] + later[0], earlier[1] * jnp.exp(later[0])[:, None, None] + later[1])

    before = carried_in(
        (local_log, local_state),
        "prompt",
        combine,
        (jnp.zeros_like(local_log), jnp.zeros_like(local_state)),
    )
    through = combine(before, (local_log, local_state))[1]
    final_state, tail_inner, tail_proj = (
        from_root(through.astype(jnp.bfloat16), "prompt", last_index).astype(through.dtype),
        from_root(own_inner.astype(jnp.bfloat16), "prompt", last_index).astype(own_inner.dtype),
        from_root(own_proj.astype(jnp.bfloat16), "prompt", last_index).astype(own_proj.dtype),
    )
    moved_state, moved_inner = (
        from_root(final_state.astype(jnp.bfloat16), "comp", owner).astype(final_state.dtype),
        from_root(tail_inner.astype(jnp.bfloat16), "comp", owner).astype(tail_inner.dtype),
    )
    lead_inner = moved_inner.astype(jnp.bfloat16)
    group_row = head_start // heads_group
    b_start = group_row * STATE_WIDTH
    c_start = state_feats + group_row * STATE_WIDTH
    proj_select = jnp.concatenate(
        [
            lax.dynamic_slice_in_dim(completion_projections, b_start, STATE_WIDTH, 2),
            lax.dynamic_slice_in_dim(completion_projections, c_start, STATE_WIDTH, 2),
        ],
        axis=2,
    )
    kernel_select = jnp.concatenate(
        [
            lax.dynamic_slice_in_dim(conv_proj, b_start, STATE_WIDTH, 1),
            lax.dynamic_slice_in_dim(conv_proj, c_start, STATE_WIDTH, 1),
        ],
        axis=1,
    )
    lead_wide = tail_proj.astype(jnp.bfloat16)
    lead_select = jnp.concatenate(
        [
            lax.dynamic_slice_in_dim(lead_wide, b_start, STATE_WIDTH, 1),
            lax.dynamic_slice_in_dim(lead_wide, c_start, STATE_WIDTH, 1),
        ],
        axis=1,
    )
    conv_row = lax.dynamic_slice_in_dim(
        conv_inner, head_start * HEAD_WIDTH, heads_row * HEAD_WIDTH, 1
    )
    rate_row = jnp.exp(lax.dynamic_slice_in_dim(decay_log, head_start, heads_row, 0))
    step_row = jax.nn.softplus(sample_step)
    slot_count = completion_inner.shape[0]
    sample_len = completion_inner.shape[1]
    block_count = sample_len // BLOCK

    def advance(carry, block_in):
        block_out, carry_next = block_scan(
            carry, block_in[0], block_in[1], block_in[2], block_in[3], rate_row[None]
        )
        return (carry_next, block_out)

    gated_list = []
    square_list = []
    for slot in range(slot_count):
        slot_conv = causal_conv(completion_inner[slot], conv_row, lead_inner)
        proj_conv = causal_conv(proj_select[slot], kernel_select, lead_select)
        inner_blocks = slot_conv.reshape(block_count, BLOCK, 1, heads_row, HEAD_WIDTH)
        b_blocks = proj_conv[:, :STATE_WIDTH].reshape(block_count, BLOCK, 1, STATE_WIDTH)
        c_blocks = proj_conv[:, STATE_WIDTH:].reshape(block_count, BLOCK, 1, STATE_WIDTH)
        step_blocks = jnp.transpose(
            step_row[:, slot].reshape(heads_row, block_count, BLOCK), (1, 0, 2)
        )[:, None]
        block_inputs = (inner_blocks, b_blocks, c_blocks, step_blocks)
        _, block_outs = lax.scan(advance, moved_state[None], block_inputs)
        ssm_out = block_outs.reshape(sample_len, heads_row * HEAD_WIDTH)
        gated = ssm_out * jax.nn.silu(completion_gate[slot].astype(jnp.float32))
        gated_list.append(gated)
        square_list.append(jnp.sum(gated * gated, axis=1))
    square_all = jnp.stack(square_list)
    square_all = square_all + from_partner(square_all, "prompt", 0)
    scale_all = lax.rsqrt(square_all / (heads_group * HEAD_WIDTH) + EPS)
    gated_all = jnp.stack(gated_list)
    result = gated_all * scale_all[:, :, None] * norm_gain[None, None, :]
    live_rows = jnp.arange(sample_len)[None, :] < sample_length[:, None]
    return jnp.where(live_rows[:, :, None], result, 0.0).astype(jnp.bfloat16)


def solution(mesh):
    placed = (
        P("prompt", "comp"),
        P("prompt", None),
        P("comp", "prompt"),
        P("comp", None, "prompt"),
        P("comp", None, "prompt"),
        P("comp", None, None),
        P("prompt", "comp", None),
        P("comp"),
        P(),
        P(),
        P(),
        P("prompt"),
    )
    return jax.shard_map(
        local, mesh=mesh, in_specs=placed, out_specs=P("comp", None, "prompt"), check_vma=False
    )
```

profile of v0, /device:TPU:1, one launch (start us, length us, event | category | flops | bytes accessed | tf_op | source)
XLA Modules:
  0.0 410.7 jit_solution(14466374462376283287)
XLA Ops:
  7.3 4.9 %collective-permute-start = (bf16[3,1024]{1,0:T(4,128)(2,1)S(1)}, bf16[3,1024]{1,0:T(4,128)(2,1)S(1)}, u32[]{:S(2)}, u32[]{:S(2)}) collective-permute-start(bf16[3,1024]{1,0:T(4,128)(2,1)S(1)} %get-tuple-element.414), channel_id=1, source_target_pairs={{0,16},{16,32},{32,48},{48,64},{64,80},{80,96},{96,112},{112,128},... | collective-permute-start | bytes 18440 | tf_op jit(solution)/shard_map/ppermute | solution.py:21
  13.0 1.9 collective-permute-start.1
  22.2 1.6 bitcast_multiply_fusion
  30.2 46.1 %all-reduce.1 = (bf16[256]{0:T(256)(128)(2,1)S(1)}, bf16[3,1024]{1,0:T(4,128)(2,1)S(1)}, bf16[3,4096]{1,0:T(4,128)(2,1)S(1)}) all-reduce(bf16[256]{0:T(256)(128)(2,1)S(1)} %dynamic-update-slice, bf16[3,1024]{1,0:T(4,128)(2,1)S(1)} %get-tuple-element.413, ...), channel_id=2, replica_groups=mesh['prompt'=16,'comp'=16] {'prompt'}, use_global_device_ids=true, to_apply=%add | all-reduce | flops 15616 | bytes 62464
  76.4 35.3 %psum.38 = bf16[3,1024]{1,0:T(4,128)(2,1)S(1)} all-reduce(bf16[3,1024]{1,0:T(4,128)(2,1)S(1)} %broadcast_select_fusion.1), channel_id=1, replica_groups=mesh['prompt'=16,'comp'=16] {'comp'}, use_global_device_ids=true, to_apply=%region_7.8 | all-reduce | flops 3072 | bytes 12288 | tf_op jit(solution)/shard_map/psum | solution.py:49
  111.9 2.1 fusion.99
  119.7 2.4 multiply_convert_fusion.8
  122.1 21.4 %while.44 = (s32[]{:T(128)}, f32[16,64,256]{2,1,0:T(8,128)S(1)}, s32[]{:T(128)}, bf16[16,16]{1,0:T(8,128)(2,1)S(1)}, bf16[16,16,64,256]{3,2,1,0:T(8,128)(2,1)}, /*index=5*/s32[]{:T(128)}, s32[]{:T(128)}) while((s32[]{:T(128)}, f32[16,64,256]{2,1,0:T(8,128)S(1)}, s32[]{:T(128)}, bf16[16,16]{1,0:T(8,128)(2,1)S(1)}, ...), condition=%wide.region_3.4_spmd.clone, body=%wide.region_2.3_spmd.clone.sunk | while | flops 1310740 | bytes 2621713 | solution.py:44
  144.9 2.1 fusion.98
  146.9 114.7 %all-reduce.5.cloned.1.call-done = bf16[16,64,256]{2,1,0:T(8,128)(2,1)} async-done(((bf16[16,64,256]{2,1,0:T(8,128)(2,1)}), bf16[16,64,256]{2,1,0:T(8,128)(2,1)}) %all-reduce.5.cloned.1.call-update) | async-done | bytes 524304 | tf_op jit(solution)/shard_map/psum | solution.py:49
  267.0 2.1 convert_element_type.228
  269.0 2.1 convert_element_type.223
  272.4 87.0 %all-reduce.7.cloned.1.call-done = bf16[1,16,64,256]{3,2,1,0:T(8,128)(2,1)} async-done(((bf16[1,16,64,256]{3,2,1,0:T(8,128)(2,1)}), bf16[1,16,64,256]{3,2,1,0:T(8,128)(2,1)}) %all-reduce.7.cloned.1.call-update) | async-done | bytes 524304 | tf_op jit(solution)/shard_map/psum | solution.py:49
  361.8 16.0 %while.43 = (s32[]{:T(128)}, f32[1,16,64,256]{3,2,1,0:T(8,128)S(1)}, f32[2,128,1,16,64]{1,4,3,2,0:T(8,128)}, f32[1,16,1]{1,2,0:T(1,128)}, f32[2,1,16,128]{3,0,2,...) while((s32[]{:T(128)}, ...), condition=%wide.region_14.15_spmd, body=%wide.region_12.14_spmd.sunk | while | flops 514478080 | bytes 16805992 | solution.py:230
  365.0 1.6 fusion.151
  366.6 1.4 fusion.150
  373.0 1.6 fusion.151
  377.8 2.1 copy.80
  379.9 3.0 fusion.72
  383.1 8.1 %while.42 = (s32[]{:T(128)}, f32[1,16,64,256]{3,2,1,0:T(8,128)S(1)}, f32[2,128,1,16,64]{1,4,3,2,0:T(8,128)S(1)}, f32[1,16,1]{1,2,0:T(1,128)}, f32[2,1,16,128]{3,...) while((s32[]{:T(128)}, ...), condition=%wide.region_11.12_spmd, body=%wide.region_9.11_spmd.sunk | while | flops 514478080 | bytes 7893013 | solution.py:230
  393.5 2.3 collective-permute-start.2
  395.8 2.2 fusion.71
  398.1 3.6 fusion.70
  401.7 2.5 copy.86
  (198 shorter events, 73.1 us)
Async XLA Ops:
  6.5 115.6 %all-gather.4.cloned.1.call-start = ((), (), s32[]{:S(2)}) async-start(), calls=%async_computation.2 | async-start | bytes 8912896 | tf_op jit(solution)/shard_map/all_gather | solution.py:27
  7.3 14.4 %collective-permute-start = (bf16[3,1024]{1,0:T(4,128)(2,1)S(1)}, bf16[3,1024]{1,0:T(4,128)(2,1)S(1)}, u32[]{:S(2)}, u32[]{:S(2)}) collective-permute-start(bf16[3,1024]{1,0:T(4,128)(2,1)S(1)} %get-tuple-element.414), channel_id=1, source_target_pairs={{0,16},{16,32},{32,48},{48,64},{64,80},{80,96},{96,112},{112,128},... | collective-permute-start | bytes 18440 | tf_op jit(solution)/shard_map/ppermute | solution.py:21
  13.0 10.9 %collective-permute-start.1 = (bf16[3,2048]{1,0:T(4,128)(2,1)S(1)}, bf16[3,2048]{1,0:T(4,128)(2,1)S(1)}, u32[]{:S(2)}, u32[]{:S(2)}) collective-permute-start(bf16[3,2048]{1,0:T(4,128)(2,1)S(1)} %slice.215), channel_id=1, source_target_pairs={{0,16},{16,32},{32,48},{48,64},{64,80},{80,96},{96,112},{112,128},... | collective-permute-start | bytes 36872 | tf_op jit(solution)/shard_map/ppermute | solution.py:21
  27.5 234.1 %all-reduce.5.cloned.1.call-start = ((), (), s32[]{:S(2)}) async-start(), calls=%async_computation | async-start | bytes 1048576 | tf_op jit(solution)/shard_map/psum | solution.py:49
  144.6 117.8 %copy-start.17 = (s32[2]{0:T(128)S(1)}, s32[2]{0:T(128)}, u32[]{:S(2)}) copy-start(s32[2]{0:T(128)} %param.25) | copy-start | bytes 28
  144.6 214.8 %all-reduce.7.cloned.1.call-start = ((), (), s32[]{:S(2)}) async-start(), calls=%async_computation.1 | async-start | bytes 1048576 | tf_op jit(solution)/shard_map/psum | solution.py:49
  264.1 2.0 copy-start.11
  264.9 4.1 copy-start
  267.0 4.8 %copy-start.12 = (bf16[256,512]{1,0:T(8,128)(2,1)S(1)}, bf16[256,512]{1,0:T(8,128)(2,1)}, u32[]{:S(2)}) copy-start(bf16[256,512]{1,0:T(8,128)(2,1)} %get-tuple-element.444) | copy-start | bytes 786436
  364.7 3.3 copy-start.7
  365.0 3.2 copy-start.2
  365.0 3.3 copy-start.6
  372.7 3.3 copy-start.7
  373.0 3.2 copy-start.2
  373.0 3.2 copy-start.6
  377.8 2.1 copy-start.1
  379.9 3.2 copy-start.13
  384.3 2.3 copy-start.5
  388.4 2.3 copy-start.5
  391.2 1.9 copy-start.9
  393.5 4.6 %copy-start.8 = (f32[1,256,1024]{1,0,2:T(1,128)S(1)}, f32[1,256,1024]{1,0,2:T(1,128)}, u32[]{:S(2)}) copy-start(f32[1,256,1024]{1,0,2:T(1,128)} %fusion.72) | copy-start | bytes 3145732
  393.5 4.6 %copy-start.15 = (f32[1024]{0:T(1024)S(1)}, f32[1024]{0:T(1024)}, u32[]{:S(2)}) copy-start(f32[1024]{0:T(1024)} %param.29) | copy-start | bytes 12292
  393.5 4.6 %copy-start.16 = (pred[2,256]{1,0:T(4,128)(4,1)S(1)}, pred[2,256]{1,0:T(4,128)(4,1)}, u32[]{:S(2)}) copy-start(pred[2,256]{1,0:T(4,128)(4,1)} %iota_compare_fusion.2) | copy-start | bytes 1540
  393.5 4.5 %collective-permute-start.2 = (f32[2,256]{1,0:T(2,128)S(1)}, f32[2,256]{1,0:T(2,128)S(1)}, u32[]{:S(2)}, u32[]{:S(2)}) collective-permute-start(f32[2,256]{1,0:T(2,128)S(1)} %pad_maximum_fusion.4), channel_id=1, source_target_pairs={{0,16},{16,0},{32,48},{48,32},{64,80},{80,64},{96,112},{112,96},{1... | collective-permute-start | bytes 6152 | tf_op jit(solution)/shard_map/ppermute | solution.py:59
  (7 other events, 8.9 us)
Sparse Core Ops, SparseCore 0:
  27.6 58.7 all-gather.3
  144.7 116.7 all-reduce.4
  265.1 94.3 all-reduce.6
where the time goes:
time: 413 us; the launch traced here: 411 us
  waiting for transfers between devices  202 us (49%)
  blocking collectives  81.4 us (20%)
  other arithmetic  59.8 us (14%)
  local copies, waits for them, and re-layouts  29 us (7%)
  between operations  14.3 us (3%)
  matrix products  14.2 us (3%)
  starting transfers between devices  9.41 us (2%)
    psum x2, waiting for transfers between devices, from_root(): return lax.psum(jnp.where(mine, array, jnp.zeros_like(array)), axis)  202 us
    unnamed x1, blocking collectives  46.1 us
    psum x1, blocking collectives, from_root(): return lax.psum(jnp.where(mine, array, jnp.zeros_like(array)), axis)  35.3 us
    select_n x16, other arithmetic, hop(): return jax.tree.map(lambda a, b: jnp.where(reached, a, b), new, before)  20.7 us
  transfers between devices with their start and end apart: 6, of which 2 were waited for; matrix products, arithmetic and copies ran while one was open for 9% of the time, Pallas kernels for 0%

commit v1 on v0

v1 whole, which is shorter than its diff:
```python
import functools

import jax
import jax.numpy as jnp
from jax import lax
from jax.experimental import pallas as pl
from jax.experimental.pallas import tpu as pltpu
from jax.sharding import PartitionSpec as P

STATE_HEADS = 256
HEAD_WIDTH = 64
STATE_WIDTH = 256
STATE_GROUPS = 8
CONV = 4
EPS = 1e-05
LOG2E = 1.4426950408889634

MESH = pl.DeviceIdType.MESH
F32 = jnp.float32
BF16 = jnp.bfloat16

ROWS = 16
COLS = 16
CHIPS = 8
TOK = 256
FEAT = 1024
HALF = 512
GROUP_HEADS = 32
PROJ_C = STATE_GROUPS * STATE_WIDTH

R_SIB, R_HALO, R_TAIL, R_RED, R_LOG, R_AG, R_SQ = 0, 3, 5, 8, 16, 24, 40
N_RECV = 42
S_SIB, S_HALO, S_TX, S_TB, S_TC, S_RED, S_LOG, S_AG, S_SQ = 0, 3, 7, 23, 38, 53, 61, 69, 84
N_SEND = 86
(L_PX, L_PB, L_PS, L_WX, L_WB, L_CX, L_CG, L_CB, L_CC, L_SS, L_WCX, L_WCB, L_WCC, L_TX, L_TB, L_TC, L_OUT) = range(17)
N_LOCAL = 18


def silu(v):
    h = 0.5 * v
    return h + h * jnp.tanh(h)


def softplus(v):
    return jnp.maximum(v, 0.0) + jnp.log1p(jnp.exp(-jnp.abs(v)))


def split3(v):
    a = v.astype(BF16)
    r = v - a.astype(F32)
    b = r.astype(BF16)
    c = (r - b.astype(F32)).astype(BF16)
    return a, b, c


def dot_nt(a, b):
    return lax.dot_general(a, b, (((1,), (1,)), ((), ())), preferred_element_type=F32)


def dot_tn(a, b):
    return lax.dot_general(a, b, (((0,), (0,)), ((), ())), preferred_element_type=F32)


def causal_conv(src, lead, taps):
    x = jnp.concatenate([lead.astype(F32)[8:], src.astype(F32)], axis=0)
    total = x * taps[3:4]
    for lag in (1, 2, 3):
        total = total + pltpu.roll(x, lag, 0) * taps[3 - lag : 4 - lag]
    return silu(total[8:])


def pick_rows(row, first, count):
    lanes = lax.broadcasted_iota(jnp.int32, (count, row.shape[1]), 1)
    heads = first + lax.broadcasted_iota(jnp.int32, (count, row.shape[1]), 0)
    wide = jnp.broadcast_to(row, (count, row.shape[1]))
    return jnp.sum(jnp.where(lanes == heads, wide, 0.0), axis=1, keepdims=True)


def kernel(
    inner, proj, pstep, cin, gate, cproj, sstep, slen, dlog, cvi, cvp, gain, out,
    px, pb, ps, hx, hb, wx, wb, cx, cg, cbc, ss, wcx, wcbc, tx, tbc,
    st, logs, red, redlog, stf, xcv, bcv, part, coef, scores, sq, sqs, obuf,
    lsem, ssem, rsem,
):
    p = lax.axis_index("prompt")
    c = lax.axis_index("comp")
    z = p // 2
    k = p % 2
    other = 1 - k
    group_col = c // 2
    group_row = p // 2
    kk = c // 8

    def ds(start, size):
        return pl.ds(pl.multiple_of(start, size), size)

    def local(src, dst, sem):
        copy = pltpu.make_async_copy(src, dst, lsem.at[sem])
        copy.start()
        return copy

    def remote(src, dst, send, recv, row, col):
        return pltpu.make_async_remote_copy(
            src_ref=src, dst_ref=dst, send_sem=ssem.at[send], recv_sem=rsem.at[recv],
            device_id=(row, col), device_id_type=MESH,
        )

    def arrived(dst, recv):
        remote(dst, dst, 0, recv, p, c).wait_recv()

    def sent(src, send):
        remote(src, src, send, 0, p, c).wait_send()

    b_col = group_col * STATE_WIDTH
    b_row = group_row * STATE_WIDTH
    copies = {}
    copies[L_PS] = local(pstep.at[ds(8 * k, 8), :], ps.at[k], L_PS)
    copies[L_PX] = local(inner.at[:, ds(k * HALF, HALF)], px.at[k], L_PX)
    copies[L_PB] = local(proj.at[:, ds(b_col, STATE_WIDTH)], pb.at[k], L_PB)
    copies[L_WX] = local(cvi.at[:, ds(c * FEAT + k * HALF, HALF)], wx, L_WX)
    copies[L_WB] = local(cvp.at[:, ds(b_col, STATE_WIDTH)], wb, L_WB)
    copies[L_SS] = local(sstep, ss, L_SS)
    copies[L_CG] = local(gate, cg, L_CG)
    copies[L_CX] = local(cin, cx, L_CX)
    copies[L_CB] = local(cproj.at[:, :, ds(b_row, STATE_WIDTH)], cbc.at[0], L_CB)
    copies[L_CC] = local(cproj.at[:, :, ds(PROJ_C + b_row, STATE_WIDTH)], cbc.at[1], L_CC)
    copies[L_WCX] = local(cvi.at[:, ds(p * FEAT, FEAT)], wcx, L_WCX)
    copies[L_WCB] = local(cvp.at[:, ds(b_row, STATE_WIDTH)], wcbc.at[0], L_WCB)
    copies[L_WCC] = local(cvp.at[:, ds(PROJ_C + b_row, STATE_WIDTH)], wcbc.at[1], L_WCC)

    barrier = pltpu.get_barrier_semaphore()

    def greet(row, col):
        pl.semaphore_signal(barrier, inc=1, device_id=(row, col), device_id_type=MESH)

    tail_self = jnp.logical_and(p == ROWS - 1, c == COLS - 1)
    red_self = jnp.logical_and(p == c, kk == k)
    greet(p + 1 - 2 * k, c)

    @pl.when(z > 0)
    def _():
        greet(2 * z - 1, c)

    for chip in range(CHIPS):
        @pl.when(jnp.logical_not(jnp.logical_and(red_self, z == chip)))
        def _():
            greet(2 * chip + kk, p)

    for step in range(1, COLS):
        greet(p, lax.rem(c + step, COLS))

    @pl.when(jnp.logical_not(tail_self))
    def _():
        greet(ROWS - 1, p)

    @pl.when(p < ROWS - 1)
    def _():
        greet(ROWS - 1, c)

    last_row = (p == ROWS - 1).astype(jnp.int32)
    halo_out = jnp.logical_and(k == 1, p < ROWS - 1)
    expected = (
        1 + 2 * halo_out.astype(jnp.int32) + CHIPS - red_self.astype(jnp.int32) + COLS - 1
        + last_row * (COLS + ROWS - 1) - tail_self.astype(jnp.int32)
    )
    pl.semaphore_wait(barrier, expected)

    sib = p + 1 - 2 * k
    sib_copies = [
        remote(pstep.at[ds(8 * other, 8), :], ps.at[k], S_SIB, R_SIB, sib, c),
        remote(inner.at[:, ds(other * HALF, HALF)], px.at[k], S_SIB + 1, R_SIB + 1, sib, c),
        remote(proj.at[:, ds(b_col, STATE_WIDTH)], pb.at[k], S_SIB + 2, R_SIB + 2, sib, c),
    ]

    def halo_copies():
        found = []
        for core in range(2):
            found.append(
                remote(
                    inner.at[pl.ds(TOK - 16, 16), pl.ds(core * HALF, HALF)], hx,
                    S_HALO + 2 * core, R_HALO, p + 1 + core, c,
                )
            )
            found.append(
                remote(
                    proj.at[pl.ds(TOK - 16, 16), ds(b_col, STATE_WIDTH)], hb,
                    S_HALO + 2 * core + 1, R_HALO + 1, p + 1 + core, c,
                )
            )
        return found

    @pl.when(halo_out)
    def _():
        for copy in halo_copies():
            copy.start()

    for copy in sib_copies:
        copy.start()

    @pl.when(z == 0)
    def _():
        hx[...] = jnp.zeros_like(hx)
        hb[...] = jnp.zeros_like(hb)

    tail_rows = pl.ds(TOK - 16, 16)

    def tail_inner(j):
        return remote(inner.at[tail_rows, :], tx, S_TX + j, R_TAIL, c, j)

    def tail_b(j):
        cols = ds((j // 2) * STATE_WIDTH, STATE_WIDTH)
        return remote(proj.at[tail_rows, cols], tbc.at[0], S_TB + j, R_TAIL + 1, j, c)

    def tail_c(j):
        cols = ds(PROJ_C + (j // 2) * STATE_WIDTH, STATE_WIDTH)
        return remote(proj.at[tail_rows, cols], tbc.at[1], S_TC + j, R_TAIL + 2, j, c)

    @pl.when(p == ROWS - 1)
    def _():
        for j in range(COLS):
            @pl.when(jnp.logical_not(jnp.logical_and(c == COLS - 1, j == COLS - 1)))
            def _():
                tail_inner(j).start()

        @pl.when(c == COLS - 1)
        def _():
            local(inner.at[tail_rows, :], tx, L_TX)

        for j in range(ROWS - 1):
            tail_b(j).start()
            tail_c(j).start()
        local(proj.at[tail_rows, ds(b_row, STATE_WIDTH)], tbc.at[0], L_TB)
        local(proj.at[tail_rows, ds(PROJ_C + b_row, STATE_WIDTH)], tbc.at[1], L_TC)

    row_id = lax.broadcasted_iota(jnp.int32, (TOK, TOK), 0)
    col_id = lax.broadcasted_iota(jnp.int32, (TOK, TOK), 1)
    tri = jnp.where(col_id <= row_id, 1.0, 0.0).astype(BF16)

    def running(values):
        a, b, d = split3(values)
        return dot_nt(a, tri) + (dot_nt(b, tri) + dot_nt(d, tri))

    def running_t(values):
        a, b, d = split3(values)
        return dot_nt(tri, a) + (dot_nt(tri, b) + dot_nt(tri, d))

    copies[L_SS].wait()
    rate_row = jnp.exp(pick_rows(dlog[...], p * 16, 16)) * LOG2E
    log_step = []
    raw = []
    for slot in range(2):
        dt = softplus(ss[:, slot, :])
        raw.append(-rate_row * dt)
        log_step.append(jnp.log2(dt))
    raw = jnp.concatenate(raw, axis=0)
    cum = running(raw)
    cum_t = running_t(raw)
    shifted = cum - jnp.concatenate(log_step, axis=0)

    copies[L_PS].wait()
    arrived(ps.at[other], R_SIB)
    rate_col = jnp.exp(pick_rows(dlog[...], c * 16 + 8 * k, 8)) * LOG2E
    dts = [softplus(ps[block]) for block in range(2)]
    cums = running(jnp.concatenate([-rate_col * dt for dt in dts], axis=0))
    cum0, cum1 = cums[:8], cums[8:]
    tot0, tot1 = cum0[:, TOK - 1 :], cum1[:, TOK - 1 :]
    weights = [jnp.exp2(tot0 - cum0 + tot1) * dts[0], jnp.exp2(tot1 - cum1) * dts[1]]
    total = jnp.broadcast_to(tot0 + tot1, (8, 128))
    for i in range(8):
        logs[i] = jnp.broadcast_to(total[i : i + 1], (8, 128))

    def red_dest(i):
        return 8 * k + i

    def own(i):
        return jnp.logical_and(p == c, red_dest(i) == c)

    def log_copy(i):
        return remote(logs.at[i], redlog.at[z], S_LOG + i, R_LOG + z, c, red_dest(i))

    def red_copy(i):
        return remote(
            st.at[pl.ds(i * HEAD_WIDTH, HEAD_WIDTH), :], red.at[z], S_RED + i, R_RED + z, c, red_dest(i)
        )

    for i in range(8):
        @pl.when(jnp.logical_not(own(i)))
        def _():
            log_copy(i).start()

        @pl.when(own(i))
        def _():
            redlog[z] = logs[i]

    spread = jnp.where(
        lax.broadcasted_iota(jnp.int32, (8, HALF), 1) // HEAD_WIDTH
        == lax.broadcasted_iota(jnp.int32, (8, HALF), 0),
        1.0,
        0.0,
    ).astype(BF16)
    spread3 = jnp.concatenate([spread.astype(F32)] * 3, axis=0).astype(BF16)
    weights3 = [
        jnp.concatenate([part_.astype(F32) for part_ in split3(w)], axis=0).astype(BF16) for w in weights
    ]

    copies[L_PB].wait()
    copies[L_WB].wait()
    copies[L_PX].wait()
    copies[L_WX].wait()

    @pl.when(z > 0)
    def _():
        arrived(hx, R_HALO)
        arrived(hb, R_HALO + 1)

    arrived(pb.at[other], R_SIB + 2)
    arrived(px.at[other], R_SIB + 1)

    taps_b = wb[...].astype(F32)
    bb = [
        causal_conv(pb[0], hb[...], taps_b).astype(BF16),
        causal_conv(pb[1], pb[0, pl.ds(TOK - 16, 16), :], taps_b).astype(BF16),
    ]
    for pair in range(4):
        cols = pl.ds(pair * 128, 128)
        taps = wx[:, cols].astype(F32)
        acc = None
        for block in range(2):
            lead = hx[:, cols] if block == 0 else px[0, pl.ds(TOK - 16, 16), cols]
            x = causal_conv(px[block, :, cols], lead, taps)
            wide = dot_tn(weights3[block], spread3[:, pair * 128 : pair * 128 + 128])
            made = dot_tn((x * wide).astype(BF16), bb[block])
            acc = made if acc is None else acc + made
        st[pl.ds(pair * 128, 128), :] = acc.astype(BF16)
        for i in (2 * pair, 2 * pair + 1):
            @pl.when(jnp.logical_not(own(i)))
            def _():
                red_copy(i).start()

            @pl.when(own(i))
            def _():
                red[z] = st[pl.ds(i * HEAD_WIDTH, HEAD_WIDTH), :]

    copies[L_CB].wait()
    copies[L_CC].wait()
    copies[L_WCB].wait()
    copies[L_WCC].wait()
    copies[L_WCX].wait()
    copies[L_CX].wait()
    copies[L_CG].wait()

    @pl.when(jnp.logical_not(tail_self))
    def _():
        arrived(tx, R_TAIL)

    @pl.when(tail_self)
    def _():
        pltpu.make_async_copy(inner.at[tail_rows, :], tx, lsem.at[L_TX]).wait()

    @pl.when(p < ROWS - 1)
    def _():
        arrived(tbc.at[0], R_TAIL + 1)
        arrived(tbc.at[1], R_TAIL + 2)

    @pl.when(p == ROWS - 1)
    def _():
        pltpu.make_async_copy(proj.at[tail_rows, ds(b_row, STATE_WIDTH)], tbc.at[0], lsem.at[L_TB]).wait()
        pltpu.make_async_copy(proj.at[tail_rows, ds(b_row, STATE_WIDTH)], tbc.at[1], lsem.at[L_TC]).wait()

    for slot in range(2):
        for which in range(2):
            bcv[which, slot] = causal_conv(
                cbc[which, slot], tbc[which], wcbc[which].astype(F32)
            ).astype(BF16)
        scores[slot] = dot_nt(bcv[1, slot], bcv[0, slot])

    lane_low = lax.broadcasted_iota(jnp.int32, (TOK, 128), 1) < HEAD_WIDTH
    causal = (
        lax.broadcasted_iota(jnp.int32, (128, 128), 1) <= lax.broadcasted_iota(jnp.int32, (128, 128), 0)
    )

    def intra(slot, pair):
        cols = pl.ds(pair * 128, 128)
        x = causal_conv(cx[slot, :, cols], tx[:, cols], wcx[:, cols].astype(F32)).astype(BF16)
        made = []
        spread_logs = []
        for h in (2 * pair, 2 * pair + 1):
            at = slot * 16 + h
            down = jnp.broadcast_to(cum_t[:, at : at + 1], (TOK, 128))
            left = down - shifted[at : at + 1, :128]
            right = down[128:] - shifted[at : at + 1, 128:]
            top = jnp.exp2(jnp.where(causal, left[:128], -jnp.inf)) * scores[slot, :128, :128]
            low = jnp.exp2(left[128:]) * scores[slot, 128:, :128]
            diag = jnp.exp2(jnp.where(causal, right, -jnp.inf)) * scores[slot, 128:, 128:]
            y0 = jnp.dot(top.astype(BF16), x[:128], preferred_element_type=F32)
            y1 = jnp.dot(low.astype(BF16), x[:128], preferred_element_type=F32) + jnp.dot(
                diag.astype(BF16), x[128:], preferred_element_type=F32
            )
            made.append(jnp.concatenate([y0, y1], axis=0))
            spread_logs.append(down)
        g = silu(cg[slot, :, cols].astype(F32))
        part[slot, :, cols] = jnp.where(lane_low, made[0], made[1]) * g
        coef[slot, :, cols] = jnp.exp2(jnp.where(lane_low, spread_logs[0], spread_logs[1])) * g

    work = [(slot, pair) for slot in range(2) for pair in range(8)]
    for slot, pair in work[:10]:
        intra(slot, pair)

    for chip in range(CHIPS):
        @pl.when(jnp.logical_not(jnp.logical_and(red_self, z == chip)))
        def _():
            arrived(redlog.at[chip], R_LOG + chip)
            arrived(red.at[chip], R_RED + chip)

    later = jnp.zeros((8, 128), F32)
    state = None
    for chip in range(CHIPS - 1, -1, -1):
        scale = jnp.exp2(later)[:1, :1]
        term = red[chip].astype(F32) * scale
        state = term if state is None else state + term
        later = later + redlog[chip]
    mine = ds(c * HEAD_WIDTH, HEAD_WIDTH)
    stf[mine, :] = state.astype(BF16)

    def ag_copy(step):
        return remote(stf.at[mine, :], stf.at[mine, :], S_AG + step - 1, R_AG + c, p, lax.rem(c + step, COLS))

    for step in range(1, COLS):
        ag_copy(step).start()

    for slot, pair in work[10:]:
        intra(slot, pair)

    for step in range(1, COLS):
        source = lax.rem(c + step, COLS)
        arrived(stf.at[ds(source * HEAD_WIDTH, HEAD_WIDTH), :], R_AG + source)

    def sq_copy(slot):
        return remote(sq.at[slot], sqs.at[slot], S_SQ + slot, R_SQ + slot, sib, c)

    for slot in range(2):
        squares = jnp.zeros((TOK, 128), F32)
        for chunk in range(4):
            cols = pl.ds(chunk * 256, 256)
            read = dot_nt(bcv[1, slot], stf[cols, :])
            gated = part[slot, :, cols] + coef[slot, :, cols] * read
            part[slot, :, cols] = gated
            squares = squares + gated[:, :128] * gated[:, :128] + gated[:, 128:] * gated[:, 128:]
        sq[slot] = squares
        sq_copy(slot).start()

    gains = gain[...]
    position = lax.broadcasted_iota(jnp.int32, (TOK, 1), 0)
    outs = []
    for slot in range(2):
        arrived(sqs.at[slot], R_SQ + slot)
        mean = jnp.sum(sq[slot] + sqs[slot], axis=1, keepdims=True) * (1.0 / (GROUP_HEADS * HEAD_WIDTH))
        scale = jnp.where(position < slen[slot], lax.rsqrt(mean + EPS), 0.0)
        obuf[slot] = (part[slot] * scale * gains).astype(BF16)
        copy = pltpu.make_async_copy(obuf.at[slot], out.at[slot], lsem.at[L_OUT + slot])
        copy.start()
        outs.append(copy)

    for copy in sib_copies:
        copy.wait_send()

    @pl.when(halo_out)
    def _():
        for copy in halo_copies():
            copy.wait_send()

    @pl.when(p == ROWS - 1)
    def _():
        for j in range(COLS):
            @pl.when(jnp.logical_not(jnp.logical_and(c == COLS - 1, j == COLS - 1)))
            def _():
                tail_inner(j).wait_send()
        for j in range(ROWS - 1):
            tail_b(j).wait_send()
            tail_c(j).wait_send()

    for i in range(8):
        @pl.when(jnp.logical_not(own(i)))
        def _():
            log_copy(i).wait_send()
            red_copy(i).wait_send()

    for step in range(1, COLS):
        ag_copy(step).wait_send()
    for slot in range(2):
        sq_copy(slot).wait_send()
    for copy in outs:
        copy.wait()


def local(
    prompt_inner,
    prompt_proj,
    prompt_step,
    completion_inner,
    completion_gate,
    completion_projections,
    sample_step,
    sample_length,
    decay_log,
    conv_inner,
    conv_proj,
    norm_gain,
):
    hbm = pl.BlockSpec(memory_space=pl.ANY)
    vmem = pl.BlockSpec(memory_space=pltpu.VMEM)
    smem = pl.BlockSpec(memory_space=pltpu.SMEM)
    V = pltpu.VMEM
    return pl.pallas_call(
        kernel,
        out_shape=jax.ShapeDtypeStruct(completion_inner.shape, BF16),
        in_specs=[hbm, hbm, hbm, hbm, hbm, hbm, hbm, smem, vmem, hbm, hbm, vmem],
        out_specs=hbm,
        scratch_shapes=[
            V((2, TOK, HALF), BF16),
            V((2, TOK, STATE_WIDTH), BF16),
            V((2, 8, TOK), F32),
            V((16, HALF), BF16),
            V((16, STATE_WIDTH), BF16),
            V((CONV, HALF), BF16),
            V((CONV, STATE_WIDTH), BF16),
            V((2, TOK, FEAT), BF16),
            V((2, TOK, FEAT), BF16),
            V((2, 2, TOK, STATE_WIDTH), BF16),
            V((16, 2, TOK), F32),
            V((CONV, FEAT), BF16),
            V((2, CONV, STATE_WIDTH), BF16),
            V((16, FEAT), BF16),
            V((2, 16, STATE_WIDTH), BF16),
            V((HALF, STATE_WIDTH), BF16),
            V((8, 8, 128), F32),
            V((CHIPS, HEAD_WIDTH, STATE_WIDTH), BF16),
            V((CHIPS, 8, 128), F32),
            V((FEAT, STATE_WIDTH), BF16),
            V((8, 128), BF16),
            V((2, 2, TOK, STATE_WIDTH), BF16),
            V((2, TOK, FEAT), F32),
            V((2, TOK, FEAT), F32),
            V((2, TOK, TOK), F32),
            V((2, TOK, 128), F32),
            V((2, TOK, 128), F32),
            V((2, TOK, FEAT), BF16),
            pltpu.SemaphoreType.DMA((N_LOCAL,)),
            pltpu.SemaphoreType.DMA((N_SEND,)),
            pltpu.SemaphoreType.DMA((N_RECV,)),
        ],
        compiler_params=pltpu.CompilerParams(
            collective_id=0, has_side_effects=True, vmem_limit_bytes=48 << 20
        ),
        name="layer",
    )(
        prompt_inner,
        prompt_proj,
        prompt_step,
        completion_inner,
        completion_gate,
        completion_projections,
        sample_step,
        sample_length,
        decay_log.reshape(1, STATE_HEADS),
        conv_inner,
        conv_proj,
        norm_gain.reshape(1, FEAT),
    )


def solution(mesh):
    placed = (
        P("prompt", "comp"),
        P("prompt", None),
        P("comp", "prompt"),
        P("comp", None, "prompt"),
        P("comp", None, "prompt"),
        P("comp", None, None),
        P("prompt", "comp", None),
        P("comp"),
        P(),
        P(),
        P(),
        P("prompt"),
    )
    return jax.shard_map(
        local, mesh=mesh, in_specs=placed, out_specs=P("comp", None, "prompt"), check_vma=False
    )
```

time: 413 us -> 70.8 us (0.17)
  waiting for transfers between devices: 202 us -> 0 us
  blocking collectives: 81.4 us -> 0 us
  other arithmetic: 59.8 us -> 0 us
  Pallas kernels: 0 us -> 59.1 us
  local copies, waits for them, and re-layouts: 29 us -> 11.2 us
  between operations: 14.3 us -> 0.02 us
  matrix products: 14.2 us -> 0 us
  starting transfers between devices: 9.41 us -> 0 us
    psum x2 -> x0, waiting for transfers between devices: 202 us -> none  [from_root(): return lax.psum(jnp.where(mine, array, jnp.zeros_like(array)), axis)]
    pallas_call x0 -> x1, Pallas kernels: none -> 59.1 us  [local(): pl.pallas_call(kernel, out_shape=jax.ShapeDtypeStruct(completion_inner.sh...]
    unnamed x1 -> x0, blocking collectives: 46.1 us -> none
    psum x1 -> x0, blocking collectives: 35.3 us -> none  [from_root(): return lax.psum(jnp.where(mine, array, jnp.zeros_like(array)), axis)]
    select_n x21 -> x0, other arithmetic: 23.4 us -> none  [the longest x16 20.7 us: hop(): return jax.tree.map(lambda a, b: jnp.where(reached, a, b), new, before)]
    convert_element_type x13 -> x0, other arithmetic: 15.6 us -> none  [the longest x3 5.02 us: causal_conv(): return jax.nn.silu(summed).astype(jnp.bfloat16)]
    dot_general x17 -> x0, matrix products: 14.2 us -> none  [the longest x4 5.73 us: block_scan(): jnp.einsum('jgn,jgkd->gkdn', b_blk, packed, preferred_element_type=jnp.fl...]
    mul x11 -> x0, other arithmetic: 10.9 us -> none  [the longest x2 5.24 us: local(): gated = ssm_out * jax.nn.silu(completion_gate[slot].astype(jnp.float32))]
  transfers between devices with their start and end apart: 6 -> 0, of which waited for: 2 -> 0; matrix products, arithmetic and copies ran while one was open for 9% -> 0% of each run, Pallas kernels for 0% -> 0%
where the time goes in v1:
time: 70.8 us; the launch traced here: 70.4 us
  Pallas kernels  59.1 us (83%)
  local copies, waits for them, and re-layouts  11.2 us (16%)
    pallas_call x1, Pallas kernels, local(): pl.pallas_call(kernel, out_shape=jax.ShapeDtypeStruct(completion_inner.sh...  59.1 us
    unnamed x23, local copies, waits for them, and re-layouts  11.2 us

profile of v1, /device:TPU:1, one launch (start us, length us, event | category | flops | bytes accessed | tf_op | source)
XLA Modules:
  0.0 70.4 jit_solution(10262570240277949399)
XLA Ops:
  0.0 0.0 copy-start
  0.0 1.6 %copy-done = bf16[256,4096]{1,0:T(8,128)(2,1)S(1)} copy-done((bf16[256,4096]{1,0:T(8,128)(2,1)S(1)}, bf16[256,4096]{1,0:T(8,128)(2,1)}, u32[]{:S(2)}) %copy-start) | copy-done | bytes 2097176
  1.6 0.0 copy-start.1
  1.6 1.2 %copy-done.1 = bf16[2,256,1024]{2,1,0:T(8,128)(2,1)S(1)} copy-done((bf16[2,256,1024]{2,1,0:T(8,128)(2,1)S(1)}, bf16[2,256,1024]{2,1,0:T(8,128)(2,1)}, u32[]{:S(2)}) %copy-start.1) | copy-done | bytes 1048600
  2.8 0.0 copy-start.2
  2.8 1.2 %copy-done.2 = bf16[2,256,1024]{2,1,0:T(8,128)(2,1)S(1)} copy-done((bf16[2,256,1024]{2,1,0:T(8,128)(2,1)S(1)}, bf16[2,256,1024]{2,1,0:T(8,128)(2,1)}, u32[]{:S(2)}) %copy-start.2) | copy-done | bytes 1048600
  4.0 0.0 copy-start.3
  4.0 1.0 %copy-done.3 = bf16[256,1024]{1,0:T(8,128)(2,1)S(1)} copy-done((bf16[256,1024]{1,0:T(8,128)(2,1)S(1)}, bf16[256,1024]{1,0:T(8,128)(2,1)}, u32[]{:S(2)}) %copy-start.3) | copy-done | bytes 524312
  5.1 0.0 copy-start.4
  5.1 0.9 %copy-done.4 = bf16[4,16384]{1,0:T(4,128)(2,1)S(1)} copy-done((bf16[4,16384]{1,0:T(4,128)(2,1)S(1)}, bf16[4,16384]{1,0:T(4,128)(2,1)}, u32[]{:S(2)}) %copy-start.4) | copy-done | bytes 131096
  6.0 0.0 copy-start.5
  6.0 0.8 %copy-done.5 = f32[16,2,256]{2,1,0:T(2,128)S(1)} copy-done((f32[16,2,256]{2,1,0:T(2,128)S(1)}, f32[16,2,256]{2,1,0:T(2,128)}, u32[]{:S(2)}) %copy-start.5) | copy-done | bytes 32792
  6.7 0.0 copy-start.6
  6.8 0.8 %copy-done.6 = bf16[4,4096]{1,0:T(4,128)(2,1)S(1)} copy-done((bf16[4,4096]{1,0:T(4,128)(2,1)S(1)}, bf16[4,4096]{1,0:T(4,128)(2,1)}, u32[]{:S(2)}) %copy-start.6) | copy-done | bytes 32792
  7.5 0.0 copy-start.7
  7.5 0.7 %copy-done.7 = f32[16,256]{1,0:T(8,128)S(1)} copy-done((f32[16,256]{1,0:T(8,128)S(1)}, f32[16,256]{1,0:T(8,128)}, u32[]{:S(2)}) %copy-start.7) | copy-done | bytes 16408
  8.2 0.0 copy-start.8
  8.2 0.7 copy-done.8
  8.9 0.0 copy-start.9
  8.9 0.7 copy-done.9
  9.6 0.0 copy-start.10
  9.6 0.7 copy-done.10
  10.2 59.1 %layer.1 = bf16[2,256,1024]{2,1,0:T(8,128)(2,1)S(1)} custom-call(bf16[256,1024]{1,0:T(8,128)(2,1)S(1)} %copy-done.3, bf16[256,4096]{1,0:T(8,128)(2,1)S(1)} %copy-done, f32[16,256]{1,0:T(8,128)S(1)} %copy-done.7, bf16[2,256,1024]{2,1,0:T(8,128)(2,1)S(1)} %copy-done.1, bf16[2,256,1024]{2,1,0:T(8,128)(2,1)S(1)} %copy-done.2, bf16[2,256,4096]{2,1,0:T(8,128)(2,1)} %cproj.1, ...), custom_call_target="tpu_custom_call" | custom-call | tf_op jit(solution)/shard_map/layer/pallas_call | solution.py:514
  69.4 1.0 %copy.14 = bf16[2,256,1024]{2,1,0:T(8,128)(2,1)} copy(bf16[2,256,1024]{2,1,0:T(8,128)(2,1)S(1)} %layer.1) | data formatting | bytes 2097152
Async XLA Ops:
  0.0 1.6 %copy-start = (bf16[256,4096]{1,0:T(8,128)(2,1)S(1)}, bf16[256,4096]{1,0:T(8,128)(2,1)}, u32[]{:S(2)}) copy-start(bf16[256,4096]{1,0:T(8,128)(2,1)} %proj.1) | copy-start | bytes 6291460
  1.6 1.2 %copy-start.1 = (bf16[2,256,1024]{2,1,0:T(8,128)(2,1)S(1)}, bf16[2,256,1024]{2,1,0:T(8,128)(2,1)}, u32[]{:S(2)}) copy-start(bf16[2,256,1024]{2,1,0:T(8,128)(2,1)} %cin.1) | copy-start | bytes 3145732
  2.8 1.2 %copy-start.2 = (bf16[2,256,1024]{2,1,0:T(8,128)(2,1)S(1)}, bf16[2,256,1024]{2,1,0:T(8,128)(2,1)}, u32[]{:S(2)}) copy-start(bf16[2,256,1024]{2,1,0:T(8,128)(2,1)} %gate.1) | copy-start | bytes 3145732
  4.0 1.0 %copy-start.3 = (bf16[256,1024]{1,0:T(8,128)(2,1)S(1)}, bf16[256,1024]{1,0:T(8,128)(2,1)}, u32[]{:S(2)}) copy-start(bf16[256,1024]{1,0:T(8,128)(2,1)} %inner.1) | copy-start | bytes 1572868
  5.1 0.9 %copy-start.4 = (bf16[4,16384]{1,0:T(4,128)(2,1)S(1)}, bf16[4,16384]{1,0:T(4,128)(2,1)}, u32[]{:S(2)}) copy-start(bf16[4,16384]{1,0:T(4,128)(2,1)} %cvi.1) | copy-start | bytes 393220
  6.0 0.8 %copy-start.5 = (f32[16,2,256]{2,1,0:T(2,128)S(1)}, f32[16,2,256]{2,1,0:T(2,128)}, u32[]{:S(2)}) copy-start(f32[16,2,256]{2,1,0:T(2,128)} %sstep.1) | copy-start | bytes 98308
  6.7 0.8 %copy-start.6 = (bf16[4,4096]{1,0:T(4,128)(2,1)S(1)}, bf16[4,4096]{1,0:T(4,128)(2,1)}, u32[]{:S(2)}) copy-start(bf16[4,4096]{1,0:T(4,128)(2,1)} %cvp.1) | copy-start | bytes 98308
  7.5 0.7 %copy-start.7 = (f32[16,256]{1,0:T(8,128)S(1)}, f32[16,256]{1,0:T(8,128)}, u32[]{:S(2)}) copy-start(f32[16,256]{1,0:T(8,128)} %pstep.1) | copy-start | bytes 49156
  8.2 0.7 copy-start.8
  8.9 0.7 copy-start.9
  9.6 0.7 copy-start.10

commit v2 on v1

v2 whole, which is shorter than its diff:
```python
import functools

import jax
import jax.numpy as jnp
from jax import lax
from jax.experimental import pallas as pl
from jax.experimental.pallas import tpu as pltpu
from jax.sharding import PartitionSpec as P

STATE_HEADS = 256
HEAD_WIDTH = 64
STATE_WIDTH = 256
STATE_GROUPS = 8
CONV = 4
EPS = 1e-05
LOG2E = 1.4426950408889634

MESH = pl.DeviceIdType.MESH
F32 = jnp.float32
BF16 = jnp.bfloat16

ROWS = 16
COLS = 16
CHIPS = 8
TOK = 256
FEAT = 1024
HALF = 512
GROUP_HEADS = 32
PROJ_C = STATE_GROUPS * STATE_WIDTH

EDGE = 8
HALVES = 2
PIECE = HEAD_WIDTH // HALVES

R_SIB, R_HALO, R_TAIL, R_LOG, R_MID = 0, 3, 5, 8, 16
R_RED = R_MID + CHIPS * HALVES
R_AG = R_RED + CHIPS * HALVES
R_SQ = R_AG + COLS * HALVES
N_RECV = R_SQ + 2
S_SIB, S_HALO, S_TX, S_RELAY, S_TB = 0, 3, 7, 8, 23
S_TC = S_TB + 15
S_LOG = S_TC + 15
S_MID = S_LOG + 8
S_RED = S_MID + CHIPS * HALVES
S_AG = S_RED + CHIPS * HALVES
S_SQ = S_AG + (COLS - 1) * HALVES
N_SEND = S_SQ + 2
(L_PX, L_PB, L_PS, L_WX, L_WB, L_CX, L_CG, L_CB, L_CC, L_SS, L_WCX, L_WCB, L_WCC, L_TX, L_TB, L_TC, L_OUT) = range(17)
N_LOCAL = 18


def silu(v):
    h = 0.5 * v
    return h + h * jnp.tanh(h)


def softplus(v):
    return jnp.maximum(v, 0.0) + jnp.log1p(jnp.exp(-jnp.abs(v)))


def split3(v):
    a = v.astype(BF16)
    r = v - a.astype(F32)
    b = r.astype(BF16)
    c = (r - b.astype(F32)).astype(BF16)
    return a, b, c


def dot_nt(a, b):
    return lax.dot_general(a, b, (((1,), (1,)), ((), ())), preferred_element_type=F32)


def dot_tn(a, b):
    return lax.dot_general(a, b, (((0,), (0,)), ((), ())), preferred_element_type=F32)


def convolve(x, taps):
    total = x * taps[3:4]
    for lag in (1, 2, 3):
        total = total + pltpu.roll(x, lag, 0) * taps[3 - lag : 4 - lag]
    return silu(total)


def causal_conv(src, lead, taps):
    return convolve(jnp.concatenate([lead.astype(F32), src.astype(F32)], axis=0), taps)[EDGE:]


def pick_rows(row, first, count):
    lanes = lax.broadcasted_iota(jnp.int32, (count, row.shape[1]), 1)
    heads = first + lax.broadcasted_iota(jnp.int32, (count, row.shape[1]), 0)
    wide = jnp.broadcast_to(row, (count, row.shape[1]))
    return jnp.sum(jnp.where(lanes == heads, wide, 0.0), axis=1, keepdims=True)


def kernel(
    inner, proj, pstep, cin, gate, cproj, sstep, slen, dlog, cvi, cvp, gain, out,
    px, pb, ps, hx, hb, wx, wb, cx, cg, cbc, ss, wcx, wcbc, tx, tbc,
    xw, wide, bb, st, logs, redlog, mid, red, stf, xcv, bcv, part, coef, scores, sq, sqs, obuf,
    lsem, ssem, rsem,
):
    p = lax.axis_index("prompt")
    c = lax.axis_index("comp")
    z = p // 2
    k = p % 2
    other = 1 - k
    sib = p + 1 - 2 * k
    group_col = c // 2
    group_row = p // 2
    kk = c // 8
    c_core = c % 2
    no = jnp.logical_not
    both = jnp.logical_and

    def ds(start, size):
        return pl.ds(pl.multiple_of(start, size), size)

    def local(src, dst, sem):
        copy = pltpu.make_async_copy(src, dst, lsem.at[sem])
        copy.start()
        return copy

    def remote(src, dst, send, recv, row, col):
        return pltpu.make_async_remote_copy(
            src_ref=src, dst_ref=dst, send_sem=ssem.at[send], recv_sem=rsem.at[recv],
            device_id=(row, col), device_id_type=MESH,
        )

    def arrived(dst, recv):
        remote(dst, dst, 0, recv, p, c).wait_recv()

    barrier = pltpu.get_barrier_semaphore()

    def greet(row, col):
        pl.semaphore_signal(barrier, inc=1, device_id=(row, col), device_id_type=MESH)

    tail_self = both(p == ROWS - 1, c == COLS - 1)
    log_self = both(p == c, kk == k)
    mid_self = both(kk == k, c_core == k)
    greet(sib, c)

    @pl.when(z > 0)
    def _():
        greet(2 * z - 1, c)

    for j in range(CHIPS):
        @pl.when(no(both(mid_self, c // 2 == j)))
        def _():
            greet(2 * z + kk, 2 * j + k)

    for step in range(1, CHIPS):
        greet(lax.rem(p + 2 * step, ROWS), c)

    for step in range(1, COLS):
        greet(p, lax.rem(c + step, COLS))

    for chip in range(CHIPS):
        @pl.when(no(both(log_self, z == chip)))
        def _():
            greet(2 * chip + kk, p)

    @pl.when(both(p == c, p < ROWS - 1))
    def _():
        greet(ROWS - 1, c)

    @pl.when(p < ROWS - 1)
    def _():
        greet(ROWS - 1, c)

    b_col = group_col * STATE_WIDTH
    b_row = group_row * STATE_WIDTH
    copies = {}
    copies[L_PS] = local(pstep.at[ds(8 * k, 8), :], ps.at[k], L_PS)
    copies[L_PB] = local(proj.at[:, ds(b_col, STATE_WIDTH)], pb.at[k], L_PB)
    copies[L_WB] = local(cvp.at[:, ds(b_col, STATE_WIDTH)], wb, L_WB)
    copies[L_PX] = local(inner.at[:, ds(k * HALF, HALF)], px.at[k], L_PX)
    copies[L_WX] = local(cvi.at[:, ds(c * FEAT + k * HALF, HALF)], wx, L_WX)

    last_row = (p == ROWS - 1).astype(jnp.int32)
    halo_out = both(k == 1, p < ROWS - 1)
    expected = (
        1 + 2 * halo_out.astype(jnp.int32)
        + CHIPS - mid_self.astype(jnp.int32) + CHIPS - 1 + COLS - 1 + CHIPS - log_self.astype(jnp.int32)
        + last_row * ROWS - tail_self.astype(jnp.int32)
    )
    pl.semaphore_wait(barrier, expected)

    edge_rows = pl.ds(TOK - EDGE, EDGE)
    sib_copies = [
        remote(pstep.at[ds(8 * other, 8), :], ps.at[k], S_SIB, R_SIB, sib, c),
        remote(proj.at[:, ds(b_col, STATE_WIDTH)], pb.at[k], S_SIB + 1, R_SIB + 1, sib, c),
        remote(inner.at[:, ds(other * HALF, HALF)], px.at[k], S_SIB + 2, R_SIB + 2, sib, c),
    ]

    def halo_copies():
        found = []
        for core in range(2):
            found.append(
                remote(
                    inner.at[edge_rows, pl.ds(core * HALF, HALF)], hx,
                    S_HALO + 2 * core, R_HALO, p + 1 + core, c,
                )
            )
            found.append(
                remote(
                    proj.at[edge_rows, ds(b_col, STATE_WIDTH)], hb,
                    S_HALO + 2 * core + 1, R_HALO + 1, p + 1 + core, c,
                )
            )
        return found

    @pl.when(halo_out)
    def _():
        for copy in halo_copies():
            copy.start()

    for copy in sib_copies:
        copy.start()

    @pl.when(z == 0)
    def _():
        hx[...] = jnp.zeros_like(hx)
        hb[...] = jnp.zeros_like(hb)

    def tail_copy():
        return remote(inner.at[edge_rows, :], tx, S_TX, R_TAIL, c, c)

    def relay_copy(step):
        return remote(tx, tx, S_RELAY + step - 1, R_TAIL, p, lax.rem(c + step, COLS))

    def tail_b(j):
        cols = ds((j // 2) * STATE_WIDTH, STATE_WIDTH)
        return remote(proj.at[edge_rows, cols], tbc.at[0], S_TB + j, R_TAIL + 1, j, c)

    def tail_c(j):
        cols = ds(PROJ_C + (j // 2) * STATE_WIDTH, STATE_WIDTH)
        return remote(proj.at[edge_rows, cols], tbc.at[1], S_TC + j, R_TAIL + 2, j, c)

    def tail_local():
        return pltpu.make_async_copy(inner.at[edge_rows, :], tx, lsem.at[L_TX])

    def tail_local_b():
        return pltpu.make_async_copy(proj.at[edge_rows, ds(b_row, STATE_WIDTH)], tbc.at[0], lsem.at[L_TB])

    def tail_local_c():
        return pltpu.make_async_copy(
            proj.at[edge_rows, ds(PROJ_C + b_row, STATE_WIDTH)], tbc.at[1], lsem.at[L_TC]
        )

    tail_out = both(p == ROWS - 1, c < COLS - 1)

    @pl.when(tail_out)
    def _():
        tail_copy().start()

    @pl.when(tail_self)
    def _():
        tail_local().start()

    copies[L_SS] = local(sstep, ss, L_SS)
    copies[L_CX] = local(cin, cx, L_CX)
    copies[L_WCX] = local(cvi.at[:, ds(p * FEAT, FEAT)], wcx, L_WCX)
    copies[L_CB] = local(cproj.at[:, :, ds(b_row, STATE_WIDTH)], cbc.at[0], L_CB)
    copies[L_CC] = local(cproj.at[:, :, ds(PROJ_C + b_row, STATE_WIDTH)], cbc.at[1], L_CC)
    copies[L_WCB] = local(cvp.at[:, ds(b_row, STATE_WIDTH)], wcbc.at[0], L_WCB)
    copies[L_WCC] = local(cvp.at[:, ds(PROJ_C + b_row, STATE_WIDTH)], wcbc.at[1], L_WCC)
    copies[L_CG] = local(gate, cg, L_CG)

    row_id = lax.broadcasted_iota(jnp.int32, (TOK, TOK), 0)
    col_id = lax.broadcasted_iota(jnp.int32, (TOK, TOK), 1)
    tri = jnp.where(col_id <= row_id, 1.0, 0.0).astype(BF16)

    def running(values):
        a, b, d = split3(values)
        return dot_nt(a, tri) + (dot_nt(b, tri) + dot_nt(d, tri))

    def running_t(values):
        a, b, d = split3(values)
        return dot_nt(tri, a) + (dot_nt(tri, b) + dot_nt(tri, d))

    rate_col = jnp.exp(pick_rows(dlog[...], c * 16 + 8 * k, 8)) * LOG2E
    spread = jnp.where(
        lax.broadcasted_iota(jnp.int32, (24, HALF), 1) // HEAD_WIDTH
        == lax.broadcasted_iota(jnp.int32, (24, HALF), 0) % 8,
        1.0,
        0.0,
    ).astype(BF16)

    def weigh(block):
        dt = softplus(ps[block])
        run = running(-rate_col * dt)
        total = run[:, TOK - 1 :]
        weight = jnp.exp2(total - run) * dt
        pieces = jnp.concatenate([piece.astype(F32) for piece in split3(weight)], axis=0).astype(BF16)
        wide[block] = dot_tn(pieces, spread)
        return total

    def conv_b(block):
        x = pb[block].astype(F32)
        bb[block] = convolve(x, wb[...].astype(F32)).astype(BF16)

    def conv_x(block):
        for quarter in range(4):
            cols = pl.ds(quarter * 128, 128)
            x = px[block, :, cols].astype(F32)
            xw[block, :, cols] = (convolve(x, wx[:, cols].astype(F32)) * wide[block, :, cols]).astype(BF16)

    copies[L_PS].wait()
    total_own = weigh(k)
    copies[L_PB].wait()
    copies[L_WB].wait()
    conv_b(k)
    copies[L_PX].wait()
    copies[L_WX].wait()
    conv_x(k)
    arrived(ps.at[other], R_SIB)
    total_sib = weigh(other)
    total1 = jnp.where(k == 1, total_own, total_sib)
    total_chip = jnp.broadcast_to(total_own + total_sib, (8, 128))
    for i in range(8):
        logs[i] = total_chip[i : i + 1]

    def log_dest(i):
        return 8 * k + i

    def log_own(i):
        return both(p == c, log_dest(i) == c)

    def log_copy(i):
        return remote(logs.at[i], redlog.at[z], S_LOG + i, R_LOG + z, c, log_dest(i))

    for i in range(8):
        @pl.when(no(log_own(i)))
        def _():
            log_copy(i).start()

        @pl.when(log_own(i))
        def _():
            redlog[z] = logs[i]

    arrived(pb.at[other], R_SIB + 1)
    conv_b(other)
    arrived(px.at[other], R_SIB + 2)
    conv_x(other)

    @pl.when(z > 0)
    def _():
        arrived(hx, R_HALO)
        arrived(hb, R_HALO + 1)

    for block in range(2):
        lead_b = hb[...] if block == 0 else pb[0, edge_rows, :]
        lead_x = hx[...] if block == 0 else px[0, edge_rows, :]
        bb[block, :16, :] = causal_conv(pb[block, :16, :], lead_b, wb[...].astype(F32)).astype(BF16)
        xw[block, :16, :] = (
            causal_conv(px[block, :16, :], lead_x, wx[...].astype(F32)) * wide[block, :16, :]
        ).astype(BF16)

    def mid_copy(i, half):
        rows = pl.ds(i * HEAD_WIDTH + half * PIECE, PIECE)
        return remote(
            st.at[rows, :], mid.at[c // 2, pl.ds(half * PIECE, PIECE), :],
            S_MID + 2 * i + half, R_MID + 2 * (c // 2) + half, 2 * z + c_core, 8 * k + i,
        )

    def mid_own(i):
        return both(mid_self, 8 * k + i == c)

    decay1 = jnp.exp2(jnp.broadcast_to(total1, (8, STATE_WIDTH)))
    for pair in range(4):
        cols = pl.ds(pair * 128, 128)
        first = dot_tn(xw[0, :, cols], bb[0])
        second = dot_tn(xw[1, :, cols], bb[1])
        for side in range(2):
            i = 2 * pair + side
            rows = slice(side * HEAD_WIDTH, (side + 1) * HEAD_WIDTH)
            st[pl.ds(i * HEAD_WIDTH, HEAD_WIDTH), :] = (
                first[rows] * decay1[i : i + 1] + second[rows]
            ).astype(BF16)

            @pl.when(no(mid_own(i)))
            def _():
                for half in range(HALVES):
                    mid_copy(i, half).start()

            @pl.when(mid_own(i))
            def _():
                mid[c // 2] = st[pl.ds(i * HEAD_WIDTH, HEAD_WIDTH), :]

    @pl.when(p == ROWS - 1)
    def _():
        for j in range(ROWS - 1):
            tail_b(j).start()
            tail_c(j).start()
        tail_local_b().start()
        tail_local_c().start()

    @pl.when(both(p == c, no(tail_self)))
    def _():
        arrived(tx, R_TAIL)

    @pl.when(tail_self)
    def _():
        tail_local().wait()

    @pl.when(p == c)
    def _():
        for step in range(1, COLS):
            relay_copy(step).start()

    copies[L_CB].wait()
    copies[L_CC].wait()
    copies[L_WCB].wait()
    copies[L_WCC].wait()
    copies[L_WCX].wait()
    copies[L_CX].wait()
    copies[L_CG].wait()
    for slot in range(2):
        for eighth in range(8):
            cols = pl.ds(eighth * 128, 128)
            x = cx[slot, :, cols].astype(F32)
            xcv[slot, :, cols] = convolve(x, wcx[:, cols].astype(F32)).astype(BF16)
        for which in range(2):
            x = cbc[which, slot].astype(F32)
            bcv[which, slot] = convolve(x, wcbc[which].astype(F32)).astype(BF16)

    copies[L_SS].wait()
    rate_row = jnp.exp(pick_rows(dlog[...], p * 16, 16)) * LOG2E
    log_step = []
    raw = []
    for slot in range(2):
        dt = softplus(ss[:, slot, :])
        raw.append(-rate_row * dt)
        log_step.append(jnp.log2(dt))
    raw = jnp.concatenate(raw, axis=0)
    cum = running(raw)
    cum_t = running_t(raw)
    shifted = cum - jnp.concatenate(log_step, axis=0)

    def red_copy(j, half):
        rows = pl.ds(half * PIECE, PIECE)
        return remote(
            mid.at[j, rows, :], red.at[z, rows, :],
            S_RED + 2 * j + half, R_RED + 2 * z + half, 2 * j + k, c,
        )

    for half in range(HALVES):
        rows = pl.ds(half * PIECE, PIECE)
        for j in range(CHIPS):
            @pl.when(no(both(mid_self, c // 2 == j)))
            def _():
                arrived(mid.at[j, rows, :], R_MID + 2 * j + half)

            @pl.when(z != j)
            def _():
                red_copy(j, half).start()

            @pl.when(z == j)
            def _():
                red[z, rows, :] = mid[j, rows, :]

    @pl.when(p != c)
    def _():
        arrived(tx, R_TAIL)

    @pl.when(p < ROWS - 1)
    def _():
        arrived(tbc.at[0], R_TAIL + 1)
        arrived(tbc.at[1], R_TAIL + 2)

    @pl.when(p == ROWS - 1)
    def _():
        tail_local_b().wait()
        tail_local_c().wait()

    for slot in range(2):
        xcv[slot, :16, :] = causal_conv(cx[slot, :16, :], tx[...], wcx[...].astype(F32)).astype(BF16)
        for which in range(2):
            bcv[which, slot, :16, :] = causal_conv(
                cbc[which, slot, :16, :], tbc[which], wcbc[which].astype(F32)
            ).astype(BF16)
        scores[slot] = dot_nt(bcv[1, slot], bcv[0, slot])

    lane_low = lax.broadcasted_iota(jnp.int32, (TOK, 128), 1) < HEAD_WIDTH
    causal = (
        lax.broadcasted_iota(jnp.int32, (128, 128), 1) <= lax.broadcasted_iota(jnp.int32, (128, 128), 0)
    )

    def intra(slot, pair):
        cols = pl.ds(pair * 128, 128)
        x = xcv[slot, :, cols]
        made = []
        spread_logs = []
        for h in (2 * pair, 2 * pair + 1):
            at = slot * 16 + h
            down = jnp.broadcast_to(cum_t[:, at : at + 1], (TOK, 128))
            left = down - shifted[at : at + 1, :128]
            right = down[128:] - shifted[at : at + 1, 128:]
            top = jnp.exp2(jnp.where(causal, left[:128], -jnp.inf)) * scores[slot, :128, :128]
            low = jnp.exp2(left[128:]) * scores[slot, 128:, :128]
            diag = jnp.exp2(jnp.where(causal, right, -jnp.inf)) * scores[slot, 128:, 128:]
            y0 = jnp.dot(top.astype(BF16), x[:128], preferred_element_type=F32)
            y1 = jnp.dot(low.astype(BF16), x[:128], preferred_element_type=F32) + jnp.dot(
                diag.astype(BF16), x[128:], preferred_element_type=F32
            )
            made.append(jnp.concatenate([y0, y1], axis=0))
            spread_logs.append(down)
        g = silu(cg[slot, :, cols].astype(F32))
        part[slot, :, cols] = jnp.where(lane_low, made[0], made[1]) * g
        coef[slot, :, cols] = jnp.exp2(jnp.where(lane_low, spread_logs[0], spread_logs[1])) * g

    for slot in range(2):
        for pair in range(8):
            intra(slot, pair)

    for chip in range(CHIPS):
        @pl.when(no(both(log_self, z == chip)))
        def _():
            arrived(redlog.at[chip], R_LOG + chip)

    later = jnp.zeros((1, 128), F32)
    scales = []
    for chip in range(CHIPS - 1, -1, -1):
        scales.insert(0, jnp.exp2(later)[:, :1])
        later = later + redlog[chip]

    def mine(half):
        return ds(c * HEAD_WIDTH + half * PIECE, PIECE)

    def ag_copy(step, half):
        return remote(
            stf.at[mine(half), :], stf.at[mine(half), :],
            S_AG + HALVES * (step - 1) + half, R_AG + HALVES * c + half, p, lax.rem(c + step, COLS),
        )

    for half in range(HALVES):
        rows = pl.ds(half * PIECE, PIECE)
        for chip in range(CHIPS):
            @pl.when(z != chip)
            def _():
                arrived(red.at[chip, rows, :], R_RED + 2 * chip + half)

        state = None
        for chip in range(CHIPS):
            term = red[chip, rows, :].astype(F32) * scales[chip]
            state = term if state is None else state + term
        stf[mine(half), :] = state.astype(BF16)
        for step in range(1, COLS):
            ag_copy(step, half).start()

    def sq_copy(slot):
        return remote(sq.at[slot], sqs.at[slot], S_SQ + slot, R_SQ + slot, sib, c)

    for chunk in range(4):
        for source in range(4 * chunk, 4 * chunk + 4):
            @pl.when(c != source)
            def _():
                for half in range(HALVES):
                    arrived(
                        stf.at[pl.ds(source * HEAD_WIDTH + half * PIECE, PIECE), :],
                        R_AG + HALVES * source + half,
                    )

        cols = pl.ds(chunk * 256, 256)
        for slot in range(2):
            read = dot_nt(bcv[1, slot], stf[cols, :])
            gated = part[slot, :, cols] + coef[slot, :, cols] * read
            part[slot, :, cols] = gated
            squares = gated[:, :128] * gated[:, :128] + gated[:, 128:] * gated[:, 128:]
            sq[slot] = squares if chunk == 0 else sq[slot] + squares
            if chunk == 3:
                sq_copy(slot).start()

    gains = gain[...]
    position = lax.broadcasted_iota(jnp.int32, (TOK, 1), 0)
    outs = []
    for slot in range(2):
        arrived(sqs.at[slot], R_SQ + slot)
        mean = jnp.sum(sq[slot] + sqs[slot], axis=1, keepdims=True) * (1.0 / (GROUP_HEADS * HEAD_WIDTH))
        scale = jnp.where(position < slen[slot], lax.rsqrt(mean + EPS), 0.0)
        obuf[slot] = (part[slot] * scale * gains).astype(BF16)
        copy = pltpu.make_async_copy(obuf.at[slot], out.at[slot], lsem.at[L_OUT + slot])
        copy.start()
        outs.append(copy)

    for copy in sib_copies:
        copy.wait_send()

    @pl.when(halo_out)
    def _():
        for copy in halo_copies():
            copy.wait_send()

    @pl.when(tail_out)
    def _():
        tail_copy().wait_send()

    @pl.when(p == c)
    def _():
        for step in range(1, COLS):
            relay_copy(step).wait_send()

    @pl.when(p == ROWS - 1)
    def _():
        for j in range(ROWS - 1):
            tail_b(j).wait_send()
            tail_c(j).wait_send()

    for i in range(8):
        @pl.when(no(log_own(i)))
        def _():
            log_copy(i).wait_send()

        @pl.when(no(mid_own(i)))
        def _():
            for half in range(HALVES):
                mid_copy(i, half).wait_send()

    for half in range(HALVES):
        for j in range(CHIPS):
            @pl.when(z != j)
            def _():
                red_copy(j, half).wait_send()

        for step in range(1, COLS):
            ag_copy(step, half).wait_send()
    for slot in range(2):
        sq_copy(slot).wait_send()
    for copy in outs:
        copy.wait()


def local(
    prompt_inner,
    prompt_proj,
    prompt_step,
    completion_inner,
    completion_gate,
    completion_projections,
    sample_step,
    sample_length,
    decay_log,
    conv_inner,
    conv_proj,
    norm_gain,
):
    hbm = pl.BlockSpec(memory_space=pl.ANY)
    vmem = pl.BlockSpec(memory_space=pltpu.VMEM)
    smem = pl.BlockSpec(memory_space=pltpu.SMEM)
    V = pltpu.VMEM
    return pl.pallas_call(
        kernel,
        out_shape=jax.ShapeDtypeStruct(completion_inner.shape, BF16),
        in_specs=[hbm, hbm, hbm, hbm, hbm, hbm, hbm, smem, vmem, hbm, hbm, vmem],
        out_specs=hbm,
        scratch_shapes=[
            V((2, TOK, HALF), BF16),
            V((2, TOK, STATE_WIDTH), BF16),
            V((2, 8, TOK), F32),
            V((EDGE, HALF), BF16),
            V((EDGE, STATE_WIDTH), BF16),
            V((CONV, HALF), BF16),
            V((CONV, STATE_WIDTH), BF16),
            V((2, TOK, FEAT), BF16),
            V((2, TOK, FEAT), BF16),
            V((2, 2, TOK, STATE_WIDTH), BF16),
            V((16, 2, TOK), F32),
            V((CONV, FEAT), BF16),
            V((2, CONV, STATE_WIDTH), BF16),
            V((EDGE, FEAT), BF16),
            V((2, EDGE, STATE_WIDTH), BF16),
            V((2, TOK, HALF), BF16),
            V((2, TOK, HALF), F32),
            V((2, TOK, STATE_WIDTH), BF16),
            V((HALF, STATE_WIDTH), BF16),
            V((8, 1, 128), F32),
            V((CHIPS, 1, 128), F32),
            V((CHIPS, HEAD_WIDTH, STATE_WIDTH), BF16),
            V((CHIPS, HEAD_WIDTH, STATE_WIDTH), BF16),
            V((FEAT, STATE_WIDTH), BF16),
            V((2, TOK, FEAT), BF16),
            V((2, 2, TOK, STATE_WIDTH), BF16),
            V((2, TOK, FEAT), F32),
            V((2, TOK, FEAT), F32),
            V((2, TOK, TOK), F32),
            V((2, TOK, 128), F32),
            V((2, TOK, 128), F32),
            V((2, TOK, FEAT), BF16),
            pltpu.SemaphoreType.DMA((N_LOCAL,)),
            pltpu.SemaphoreType.DMA((N_SEND,)),
            pltpu.SemaphoreType.DMA((N_RECV,)),
        ],
        compiler_params=pltpu.CompilerParams(
            collective_id=0, has_side_effects=True, vmem_limit_bytes=60 << 20
        ),
        name="layer",
    )(
        prompt_inner,
        prompt_proj,
        prompt_step,
        completion_inner,
        completion_gate,
        completion_projections,
        sample_step,
        sample_length,
        decay_log.reshape(1, STATE_HEADS),
        conv_inner,
        conv_proj,
        norm_gain.reshape(1, FEAT),
    )


def solution(mesh):
    placed = (
        P("prompt", "comp"),
        P("prompt", None),
        P("comp", "prompt"),
        P("comp", None, "prompt"),
        P("comp", None, "prompt"),
        P("comp", None, None),
        P("prompt", "comp", None),
        P("comp"),
        P(),
        P(),
        P(),
        P("prompt"),
    )
    return jax.shard_map(
        local, mesh=mesh, in_specs=placed, out_specs=P("comp", None, "prompt"), check_vma=False
    )
```

time: 70.8 us -> 42.3 us (0.60)
  Pallas kernels: 59.1 us -> 39.9 us
  local copies, waits for them, and re-layouts: 11.2 us -> 2.26 us
    pallas_call x1, Pallas kernels: 59.1 us -> 39.9 us  [local(): pl.pallas_call(kernel, out_shape=jax.ShapeDtypeStruct(completion_inner.sh...]
    unnamed x23 -> x1, local copies, waits for them, and re-layouts: 11.2 us -> 2.26 us
where the time goes in v2:
time: 42.3 us; the launch traced here: 42.2 us
  Pallas kernels  39.9 us (94%)
  local copies, waits for them, and re-layouts  2.26 us (5%)
    pallas_call x1, Pallas kernels, local(): pl.pallas_call(kernel, out_shape=jax.ShapeDtypeStruct(completion_inner.sh...  39.9 us
    unnamed x1, local copies, waits for them, and re-layouts  2.26 us

profile of v2, /device:TPU:1, one launch (start us, length us, event | category | flops | bytes accessed | tf_op | source)
XLA Modules:
  0.0 42.2 jit_solution(8236601958269925051)
XLA Ops:
  0.0 39.9 %layer.1 = bf16[2,256,1024]{2,1,0:T(8,128)(2,1)} custom-call(bf16[256,1024]{1,0:T(8,128)(2,1)} %inner.1, bf16[256,4096]{1,0:T(8,128)(2,1)} %proj.1, f32[16,256]{1,0:T(8,128)} %pstep.1, bf16[2,256,1024]{2,1,0:T(8,128)(2,1)} %cin.1, bf16[2,256,1024]{2,1,0:T(8,128)(2,1)} %gate.1, bf16[2,256,4096]{2,1,0:T(8,128)(2,1)} %cproj.1, f32[16,2,256]{2,1,0:T(2,128)} %sstep.1, ...), custom_call_target="tpu_custom_call" | custom-call | tf_op jit(solution)/shard_map/layer/pallas_call | solution.py:650
  39.9 2.3 %copy.14 = bf16[2,256,1024]{2,1,0:T(8,128)(2,1)} copy(bf16[2,256,1024]{2,1,0:T(8,128)(2,1)} %layer.1) | data formatting | bytes 2097152

commit v3 on v2

--- a/solution.py
+++ b/solution.py
@@ -32,21 +32,21 @@
 HALVES = 2
 PIECE = HEAD_WIDTH // HALVES
 
-R_SIB, R_HALO, R_TAIL, R_LOG, R_MID = 0, 3, 5, 8, 16
+R_SIB, R_HALO, R_TAIL, R_MLOG, R_LOG, R_MID = 0, 3, 5, 7, 15, 23
 R_RED = R_MID + CHIPS * HALVES
 R_AG = R_RED + CHIPS * HALVES
 R_SQ = R_AG + COLS * HALVES
 N_RECV = R_SQ + 2
 S_SIB, S_HALO, S_TX, S_RELAY, S_TB = 0, 3, 7, 8, 23
-S_TC = S_TB + 15
-S_LOG = S_TC + 15
+S_MLOG = S_TB + 15
+S_LOG = S_MLOG + 8
 S_MID = S_LOG + 8
 S_RED = S_MID + CHIPS * HALVES
 S_AG = S_RED + CHIPS * HALVES
 S_SQ = S_AG + (COLS - 1) * HALVES
 N_SEND = S_SQ + 2
-(L_PX, L_PB, L_PS, L_WX, L_WB, L_CX, L_CG, L_CB, L_CC, L_SS, L_WCX, L_WCB, L_WCC, L_TX, L_TB, L_TC, L_OUT) = range(17)
-N_LOCAL = 18
+(L_PX, L_PB, L_PS, L_WX, L_WB, L_CX, L_CG, L_CB, L_CC, L_SS, L_WCX, L_WCB, L_WCC, L_TX, L_TB, L_TC, L_LEN, L_LOG, L_GAIN, L_OUT) = range(20)
+N_LOCAL = 21
 
 
 def silu(v):
@@ -93,10 +93,10 @@
 
 
 def kernel(
-    inner, proj, pstep, cin, gate, cproj, sstep, slen, dlog, cvi, cvp, gain, out,
+    inner, proj, pstep, cin, gate, cproj, sstep, slen_in, dlog_in, cvi, cvp, gain_in, out,
     px, pb, ps, hx, hb, wx, wb, cx, cg, cbc, ss, wcx, wcbc, tx, tbc,
-    xw, wide, bb, st, logs, redlog, mid, red, stf, xcv, bcv, part, coef, scores, sq, sqs, obuf,
-    lsem, ssem, rsem,
+    trow, tpack, xw, wide, bb, base, st, logs, midlog, redlog, mid, red, stf, xcv, bcv, part, coef, scores, sq, sqs, obuf,
+    slen, dlog, gain, lsem, ssem, rsem,
 ):
     p = lax.axis_index("prompt")
     c = lax.axis_index("comp")
@@ -134,41 +134,36 @@
         pl.semaphore_signal(barrier, inc=1, device_id=(row, col), device_id_type=MESH)
 
     tail_self = both(p == ROWS - 1, c == COLS - 1)
-    log_self = both(p == c, kk == k)
     mid_self = both(kk == k, c_core == k)
-    greet(sib, c)
+    for step in (4, 3, 5, 2, 6, 1, 7):
+        greet(lax.rem(p + 2 * step, ROWS), c)
 
     @pl.when(z > 0)
     def _():
         greet(2 * z - 1, c)
+
+    @pl.when(both(p == c, p < ROWS - 1))
+    def _():
+        greet(ROWS - 1, c)
+
+    @pl.when(p < ROWS - 1)
+    def _():
+        greet(ROWS - 1, c)
 
     for j in range(CHIPS):
         @pl.when(no(both(mid_self, c // 2 == j)))
         def _():
             greet(2 * z + kk, 2 * j + k)
 
-    for step in range(1, CHIPS):
-        greet(lax.rem(p + 2 * step, ROWS), c)
-
     for step in range(1, COLS):
         greet(p, lax.rem(c + step, COLS))
 
-    for chip in range(CHIPS):
-        @pl.when(no(both(log_self, z == chip)))
-        def _():
-            greet(2 * chip + kk, p)
-
-    @pl.when(both(p == c, p < ROWS - 1))
-    def _():
-        greet(ROWS - 1, c)
-
-    @pl.when(p < ROWS - 1)
-    def _():
-        greet(ROWS - 1, c)
+    greet(sib, c)
 
     b_col = group_col * STATE_WIDTH
     b_row = group_row * STATE_WIDTH
     copies = {}
+    copies[L_LOG] = local(dlog_in, dlog, L_LOG)
     copies[L_PS] = local(pstep.at[ds(8 * k, 8), :], ps.at[k], L_PS)
     copies[L_PB] = local(proj.at[:, ds(b_col, STATE_WIDTH)], pb.at[k], L_PB)
     copies[L_WB] = local(cvp.at[:, ds(b_col, STATE_WIDTH)], wb, L_WB)
@@ -179,7 +174,7 @@
     halo_out = both(k == 1, p < ROWS - 1)
     expected = (
         1 + 2 * halo_out.astype(jnp.int32)
-        + CHIPS - mid_self.astype(jnp.int32) + CHIPS - 1 + COLS - 1 + CHIPS - log_self.astype(jnp.int32)
+        + CHIPS - mid_self.astype(jnp.int32) + CHIPS - 1 + COLS - 1
         + last_row * ROWS - tail_self.astype(jnp.int32)
     )
     pl.semaphore_wait(barrier, expected)
@@ -227,24 +222,14 @@
     def relay_copy(step):
         return remote(tx, tx, S_RELAY + step - 1, R_TAIL, p, lax.rem(c + step, COLS))
 
-    def tail_b(j):
-        cols = ds((j // 2) * STATE_WIDTH, STATE_WIDTH)
-        return remote(proj.at[edge_rows, cols], tbc.at[0], S_TB + j, R_TAIL + 1, j, c)
-
-    def tail_c(j):
-        cols = ds(PROJ_C + (j // 2) * STATE_WIDTH, STATE_WIDTH)
-        return remote(proj.at[edge_rows, cols], tbc.at[1], S_TC + j, R_TAIL + 2, j, c)
+    def tail_bc(j):
+        return remote(tpack.at[j // 2], tbc, S_TB + j, R_TAIL + 1, j, c)
 
     def tail_local():
         return pltpu.make_async_copy(inner.at[edge_rows, :], tx, lsem.at[L_TX])
 
-    def tail_local_b():
-        return pltpu.make_async_copy(proj.at[edge_rows, ds(b_row, STATE_WIDTH)], tbc.at[0], lsem.at[L_TB])
-
-    def tail_local_c():
-        return pltpu.make_async_copy(
-            proj.at[edge_rows, ds(PROJ_C + b_row, STATE_WIDTH)], tbc.at[1], lsem.at[L_TC]
-        )
+    def tail_proj():
+        return pltpu.make_async_copy(proj.at[edge_rows, :], trow, lsem.at[L_TB])
 
     tail_out = both(p == ROWS - 1, c < COLS - 1)
 
@@ -255,6 +240,10 @@
     @pl.when(tail_self)
     def _():
         tail_local().start()
+
+    @pl.when(p == ROWS - 1)
+    def _():
+        tail_proj().start()
 
     copies[L_SS] = local(sstep, ss, L_SS)
     copies[L_CX] = local(cin, cx, L_CX)
@@ -264,6 +253,8 @@
     copies[L_WCB] = local(cvp.at[:, ds(b_row, STATE_WIDTH)], wcbc.at[0], L_WCB)
     copies[L_WCC] = local(cvp.at[:, ds(PROJ_C + b_row, STATE_WIDTH)], wcbc.at[1], L_WCC)
     copies[L_CG] = local(gate, cg, L_CG)
+    copies[L_GAIN] = local(gain_in, gain, L_GAIN)
+    copies[L_LEN] = local(slen_in, slen, L_LEN)
 
     row_id = lax.broadcasted_iota(jnp.int32, (TOK, TOK), 0)
     col_id = lax.broadcasted_iota(jnp.int32, (TOK, TOK), 1)
@@ -277,6 +268,7 @@
         a, b, d = split3(values)
         return dot_nt(tri, a) + (dot_nt(tri, b) + dot_nt(tri, d))
 
+    copies[L_LOG].wait()
     rate_col = jnp.exp(pick_rows(dlog[...], c * 16 + 8 * k, 8)) * LOG2E
     spread = jnp.where(
         lax.broadcasted_iota(jnp.int32, (24, HALF), 1) // HEAD_WIDTH
@@ -312,6 +304,18 @@
     copies[L_PX].wait()
     copies[L_WX].wait()
     conv_x(k)
+
+    @pl.when(p == ROWS - 1)
+    def _():
+        tail_proj().wait()
+        for group in range(STATE_GROUPS):
+            for which in range(2):
+                first = which * PROJ_C + group * STATE_WIDTH
+                tpack[group, which] = trow[:, first : first + STATE_WIDTH]
+        tbc[...] = tpack[group_row]
+        for j in range(ROWS - 1):
+            tail_bc(j).start()
+
     arrived(ps.at[other], R_SIB)
     total_sib = weigh(other)
     total1 = jnp.where(k == 1, total_own, total_sib)
@@ -319,52 +323,33 @@
     for i in range(8):
         logs[i] = total_chip[i : i + 1]
 
-    def log_dest(i):
-        return 8 * k + i
-
-    def log_own(i):
-        return both(p == c, log_dest(i) == c)
-
-    def log_copy(i):
-        return remote(logs.at[i], redlog.at[z], S_LOG + i, R_LOG + z, c, log_dest(i))
-
-    for i in range(8):
-        @pl.when(no(log_own(i)))
-        def _():
-            log_copy(i).start()
-
-        @pl.when(log_own(i))
-        def _():
-            redlog[z] = logs[i]
-
-    arrived(pb.at[other], R_SIB + 1)
-    conv_b(other)
-    arrived(px.at[other], R_SIB + 2)
-    conv_x(other)
-
-    @pl.when(z > 0)
-    def _():
-        arrived(hx, R_HALO)
-        arrived(hb, R_HALO + 1)
-
-    for block in range(2):
-        lead_b = hb[...] if block == 0 else pb[0, edge_rows, :]
-        lead_x = hx[...] if block == 0 else px[0, edge_rows, :]
-        bb[block, :16, :] = causal_conv(pb[block, :16, :], lead_b, wb[...].astype(F32)).astype(BF16)
-        xw[block, :16, :] = (
-            causal_conv(px[block, :16, :], lead_x, wx[...].astype(F32)) * wide[block, :16, :]
-        ).astype(BF16)
-
-    def mid_copy(i, half):
-        rows = pl.ds(i * HEAD_WIDTH + half * PIECE, PIECE)
-        return remote(
-            st.at[rows, :], mid.at[c // 2, pl.ds(half * PIECE, PIECE), :],
-            S_MID + 2 * i + half, R_MID + 2 * (c // 2) + half, 2 * z + c_core, 8 * k + i,
-        )
-
     def mid_own(i):
         return both(mid_self, 8 * k + i == c)
 
+    def mlog_copy(i):
+        return remote(
+            logs.at[i], midlog.at[c // 2], S_MLOG + i, R_MLOG + c // 2, 2 * z + c_core, 8 * k + i
+        )
+
+    for i in range(8):
+        @pl.when(no(mid_own(i)))
+        def _():
+            mlog_copy(i).start()
+
+        @pl.when(mid_own(i))
+        def _():
+            midlog[c // 2] = logs[i]
+
+    arrived(pb.at[other], R_SIB + 1)
+    arrived(px.at[other], R_SIB + 2)
+    conv_b(other)
+    conv_x(other)
+
+    taps_b = wb[...].astype(F32)
+    taps_x = wx[...].astype(F32)
+    bb[1, :16, :] = causal_conv(pb[1, :16, :], pb[0, edge_rows, :], taps_b).astype(BF16)
+    xw[1, :16, :] = (causal_conv(px[1, :16, :], px[0, edge_rows, :], taps_x) * wide[1, :16, :]).astype(BF16)
+    xw[0, :16, :] = jnp.zeros((16, HALF), BF16)
     decay1 = jnp.exp2(jnp.broadcast_to(total1, (8, STATE_WIDTH)))
     for pair in range(4):
         cols = pl.ds(pair * 128, 128)
@@ -373,9 +358,30 @@
         for side in range(2):
             i = 2 * pair + side
             rows = slice(side * HEAD_WIDTH, (side + 1) * HEAD_WIDTH)
-            st[pl.ds(i * HEAD_WIDTH, HEAD_WIDTH), :] = (
-                first[rows] * decay1[i : i + 1] + second[rows]
-            ).astype(BF16)
+            base[pl.ds(i * HEAD_WIDTH, HEAD_WIDTH), :] = first[rows] * decay1[i : i + 1] + second[rows]
+
+    @pl.when(z > 0)
+    def _():
+        arrived(hx, R_HALO)
+        arrived(hb, R_HALO + 1)
+
+    edge_b = causal_conv(pb[0, :16, :], hb[...], taps_b).astype(BF16)
+    edge_x = (causal_conv(px[0, :16, :], hx[...], taps_x) * wide[0, :16, :]).astype(BF16)
+
+    def mid_copy(i, half):
+        rows = pl.ds(i * HEAD_WIDTH + half * PIECE, PIECE)
+        return remote(
+            st.at[rows, :], mid.at[c // 2, pl.ds(half * PIECE, PIECE), :],
+            S_MID + 2 * i + half, R_MID + 2 * (c // 2) + half, 2 * z + c_core, 8 * k + i,
+        )
+
+    for pair in range(4):
+        edge = dot_tn(edge_x[:, pair * 128 : pair * 128 + 128], edge_b)
+        for side in range(2):
+            i = 2 * pair + side
+            rows = slice(side * HEAD_WIDTH, (side + 1) * HEAD_WIDTH)
+            mine_i = pl.ds(i * HEAD_WIDTH, HEAD_WIDTH)
+            st[mine_i, :] = (base[mine_i, :] + edge[rows] * decay1[i : i + 1]).astype(BF16)
 
             @pl.when(no(mid_own(i)))
             def _():
@@ -385,14 +391,6 @@
             @pl.when(mid_own(i))
             def _():
                 mid[c // 2] = st[pl.ds(i * HEAD_WIDTH, HEAD_WIDTH), :]
-
-    @pl.when(p == ROWS - 1)
-    def _():
-        for j in range(ROWS - 1):
-            tail_b(j).start()
-            tail_c(j).start()
-        tail_local_b().start()
-        tail_local_c().start()
 
     @pl.when(both(p == c, no(tail_self)))
     def _():
@@ -443,6 +441,22 @@
             S_RED + 2 * j + half, R_RED + 2 * z + half, 2 * j + k, c,
         )
 
+    def log_copy(j):
+        return remote(midlog.at[j], redlog.at[z], S_LOG + j, R_LOG + z, 2 * j + k, c)
+
+    for j in range(CHIPS):
+        @pl.when(no(both(mid_self, c // 2 == j)))
+        def _():
+            arrived(midlog.at[j], R_MLOG + j)
+
+        @pl.when(z != j)
+        def _():
+            log_copy(j).start()
+
+        @pl.when(z == j)
+        def _():
+            redlog[z] = midlog[j]
+
     for half in range(HALVES):
         rows = pl.ds(half * PIECE, PIECE)
         for j in range(CHIPS):
@@ -464,13 +478,7 @@
 
     @pl.when(p < ROWS - 1)
     def _():
-        arrived(tbc.at[0], R_TAIL + 1)
-        arrived(tbc.at[1], R_TAIL + 2)
-
-    @pl.when(p == ROWS - 1)
-    def _():
-        tail_local_b().wait()
-        tail_local_c().wait()
+        arrived(tbc, R_TAIL + 1)
 
     for slot in range(2):
         xcv[slot, :16, :] = causal_conv(cx[slot, :16, :], tx[...], wcx[...].astype(F32)).astype(BF16)
@@ -513,7 +521,7 @@
             intra(slot, pair)
 
     for chip in range(CHIPS):
-        @pl.when(no(both(log_self, z == chip)))
+        @pl.when(z != chip)
         def _():
             arrived(redlog.at[chip], R_LOG + chip)
 
@@ -570,6 +578,8 @@
             if chunk == 3:
                 sq_copy(slot).start()
 
+    copies[L_GAIN].wait()
+    copies[L_LEN].wait()
     gains = gain[...]
     position = lax.broadcasted_iota(jnp.int32, (TOK, 1), 0)
     outs = []
@@ -602,16 +612,12 @@
     @pl.when(p == ROWS - 1)
     def _():
         for j in range(ROWS - 1):
-            tail_b(j).wait_send()
-            tail_c(j).wait_send()
+            tail_bc(j).wait_send()
 
     for i in range(8):
-        @pl.when(no(log_own(i)))
-        def _():
-            log_copy(i).wait_send()
-
         @pl.when(no(mid_own(i)))
         def _():
+            mlog_copy(i).wait_send()
             for half in range(HALVES):
                 mid_copy(i, half).wait_send()
 
@@ -620,6 +626,8 @@
             @pl.when(z != j)
             def _():
                 red_copy(j, half).wait_send()
+                if half == 0:
+                    log_copy(j).wait_send()
 
         for step in range(1, COLS):
             ag_copy(step, half).wait_send()
@@ -644,13 +652,11 @@
     norm_gain,
 ):
     hbm = pl.BlockSpec(memory_space=pl.ANY)
-    vmem = pl.BlockSpec(memory_space=pltpu.VMEM)
-    smem = pl.BlockSpec(memory_space=pltpu.SMEM)
     V = pltpu.VMEM
-    return pl.pallas_call(
+    layer = pl.pallas_call(
         kernel,
         out_shape=jax.ShapeDtypeStruct(completion_inner.shape, BF16),
-        in_specs=[hbm, hbm, hbm, hbm, hbm, hbm, hbm, smem, vmem, hbm, hbm, vmem],
+        in_specs=[hbm] * 12,
         out_specs=hbm,
         scratch_shapes=[
             V((2, TOK, HALF), BF16),
@@ -668,11 +674,15 @@
             V((2, CONV, STATE_WIDTH), BF16),
             V((EDGE, FEAT), BF16),
             V((2, EDGE, STATE_WIDTH), BF16),
+            V((EDGE, 2 * PROJ_C), BF16),
+            V((STATE_GROUPS, 2, EDGE, STATE_WIDTH), BF16),
             V((2, TOK, HALF), BF16),
             V((2, TOK, HALF), F32),
             V((2, TOK, STATE_WIDTH), BF16),
+            V((HALF, STATE_WIDTH), F32),
             V((HALF, STATE_WIDTH), BF16),
             V((8, 1, 128), F32),
+            V((CHIPS, 1, 128), F32),
             V((CHIPS, 1, 128), F32),
             V((CHIPS, HEAD_WIDTH, STATE_WIDTH), BF16),
             V((CHIPS, HEAD_WIDTH, STATE_WIDTH), BF16),
@@ -685,15 +695,19 @@
             V((2, TOK, 128), F32),
             V((2, TOK, 128), F32),
             V((2, TOK, FEAT), BF16),
+            pltpu.SMEM((2,), jnp.int32),
+            V((1, STATE_HEADS), F32),
+            V((1, FEAT), F32),
             pltpu.SemaphoreType.DMA((N_LOCAL,)),
             pltpu.SemaphoreType.DMA((N_SEND,)),
             pltpu.SemaphoreType.DMA((N_RECV,)),
         ],
         compiler_params=pltpu.CompilerParams(
-            collective_id=0, has_side_effects=True, vmem_limit_bytes=60 << 20
+            collective_id=0, has_side_effects=True, vmem_limit_bytes=48 << 20
         ),
         name="layer",
-    )(
+    )
+    arrays = (
         prompt_inner,
         prompt_proj,
         prompt_step,
@@ -707,6 +721,7 @@
         conv_proj,
         norm_gain.reshape(1, FEAT),
     )
+    return layer(*[pltpu.with_memory_space_constraint(array, pltpu.HBM) for array in arrays])
 
 
 def solution(mesh):

time: 42.3 us -> 39.3 us (0.929)
  Pallas kernels: 39.9 us -> 38.2 us
  local copies, waits for them, and re-layouts: 2.26 us -> 0.97 us
    pallas_call x1, Pallas kernels: 39.9 us -> 38.2 us  [local(): layer(*[pltpu.with_memory_space_constraint(array, pltpu.HBM) for array in...]
    unnamed x1, local copies, waits for them, and re-layouts: 2.26 us -> 0.97 us
where the time goes in v3:
time: 39.3 us; the launch traced here: 39.2 us
  Pallas kernels  38.2 us (97%)
  local copies, waits for them, and re-layouts  0.97 us (2%)
    pallas_call x1, Pallas kernels, local(): layer(*[pltpu.with_memory_space_constraint(array, pltpu.HBM) for array in...  38.2 us
    unnamed x1, local copies, waits for them, and re-layouts  0.97 us

profile of v3, /device:TPU:1, one launch (start us, length us, event | category | flops | bytes accessed | tf_op | source)
XLA Modules:
  0.0 39.2 jit_solution(15021038180980158258)
XLA Ops:
  0.0 38.2 %layer.1 = bf16[2,256,1024]{2,1,0:T(8,128)(2,1)S(1)} custom-call(bf16[256,1024]{1,0:T(8,128)(2,1)} %inner.1, bf16[256,4096]{1,0:T(8,128)(2,1)} %proj.1, f32[16,256]{1,0:T(8,128)} %pstep.1, bf16[2,256,1024]{2,1,0:T(8,128)(2,1)} %cin.1, bf16[2,256,1024]{2,1,0:T(8,128)(2,1)} %gate.1, bf16[2,256,4096]{2,1,0:T(8,128)(2,1)} %cproj.1, f32[16,2,256]{2,1,0:T(2,128)} %sstep.1, ...), custom_call_target="tpu_custom_call" | custom-call | tf_op jit(solution)/shard_map/layer/pallas_call | solution.py:724
  38.3 1.0 %copy.14 = bf16[2,256,1024]{2,1,0:T(8,128)(2,1)} copy(bf16[2,256,1024]{2,1,0:T(8,128)(2,1)S(1)} %layer.1) | data formatting | bytes 2097152

commit v4 on v3

--- a/solution.py
+++ b/solution.py
@@ -385,12 +385,17 @@
 
             @pl.when(no(mid_own(i)))
             def _():
-                for half in range(HALVES):
-                    mid_copy(i, half).start()
+                mid_copy(i, 0).start()
 
             @pl.when(mid_own(i))
             def _():
                 mid[c // 2] = st[pl.ds(i * HEAD_WIDTH, HEAD_WIDTH), :]
+
+    for half in range(1, HALVES):
+        for i in range(8):
+            @pl.when(no(mid_own(i)))
+            def _():
+                mid_copy(i, half).start()
 
     @pl.when(both(p == c, no(tail_self)))
     def _():
@@ -516,9 +521,9 @@
         part[slot, :, cols] = jnp.where(lane_low, made[0], made[1]) * g
         coef[slot, :, cols] = jnp.exp2(jnp.where(lane_low, spread_logs[0], spread_logs[1])) * g
 
-    for slot in range(2):
-        for pair in range(8):
-            intra(slot, pair)
+    work = [(slot, pair) for slot in range(2) for pair in range(8)]
+    for slot, pair in work[:10]:
+        intra(slot, pair)
 
     for chip in range(CHIPS):
         @pl.when(z != chip)
@@ -554,6 +559,45 @@
         stf[mine(half), :] = state.astype(BF16)
         for step in range(1, COLS):
             ag_copy(step, half).start()
+        for slot, pair in work[10 + 3 * half : 13 + 3 * half]:
+            intra(slot, pair)
+
+    for copy in sib_copies:
+        copy.wait_send()
+
+    @pl.when(halo_out)
+    def _():
+        for copy in halo_copies():
+            copy.wait_send()
+
+    @pl.when(tail_out)
+    def _():
+        tail_copy().wait_send()
+
+    @pl.when(p == c)
+    def _():
+        for step in range(1, COLS):
+            relay_copy(step).wait_send()
+
+    @pl.when(p == ROWS - 1)
+    def _():
+        for j in range(ROWS - 1):
+            tail_bc(j).wait_send()
+
+    for i in range(8):
+        @pl.when(no(mid_own(i)))
+        def _():
+            mlog_copy(i).wait_send()
+            for half in range(HALVES):
+                mid_copy(i, half).wait_send()
+
+    for half in range(HALVES):
+        for j in range(CHIPS):
+            @pl.when(z != j)
+            def _():
+                red_copy(j, half).wait_send()
+                if half == 0:
+                    log_copy(j).wait_send()
 
     def sq_copy(slot):
         return remote(sq.at[slot], sqs.at[slot], S_SQ + slot, R_SQ + slot, sib, c)
@@ -578,6 +622,9 @@
             if chunk == 3:
                 sq_copy(slot).start()
 
+    for half in range(HALVES):
+        for step in range(1, COLS):
+            ag_copy(step, half).wait_send()
     copies[L_GAIN].wait()
     copies[L_LEN].wait()
     gains = gain[...]
@@ -592,45 +639,6 @@
         copy.start()
         outs.append(copy)
 
-    for copy in sib_copies:
-        copy.wait_send()
-
-    @pl.when(halo_out)
-    def _():
-        for copy in halo_copies():
-            copy.wait_send()
-
-    @pl.when(tail_out)
-    def _():
-        tail_copy().wait_send()
-
-    @pl.when(p == c)
-    def _():
-        for step in range(1, COLS):
-            relay_copy(step).wait_send()
-
-    @pl.when(p == ROWS - 1)
-    def _():
-        for j in range(ROWS - 1):
-            tail_bc(j).wait_send()
-
-    for i in range(8):
-        @pl.when(no(mid_own(i)))
-        def _():
-            mlog_copy(i).wait_send()
-            for half in range(HALVES):
-                mid_copy(i, half).wait_send()
-
-    for half in range(HALVES):
-        for j in range(CHIPS):
-            @pl.when(z != j)
-            def _():
-                red_copy(j, half).wait_send()
-                if half == 0:
-                    log_copy(j).wait_send()
-
-        for step in range(1, COLS):
-            ag_copy(step, half).wait_send()
     for slot in range(2):
         sq_copy(slot).wait_send()
     for copy in outs:

time: 39.3 us -> 38.4 us (0.977)
  Pallas kernels: 38.2 us -> 37.4 us
    pallas_call x1, Pallas kernels: 38.2 us -> 37.4 us  [local(): layer(*[pltpu.with_memory_space_constraint(array, pltpu.HBM) for array in...]
where the time goes in v4:
time: 38.4 us; the launch traced here: 38.3 us
  Pallas kernels  37.4 us (97%)
  local copies, waits for them, and re-layouts  0.97 us (3%)
    pallas_call x1, Pallas kernels, local(): layer(*[pltpu.with_memory_space_constraint(array, pltpu.HBM) for array in...  37.4 us
    unnamed x1, local copies, waits for them, and re-layouts  0.97 us

profile of v4, /device:TPU:1, one launch (start us, length us, event | category | flops | bytes accessed | tf_op | source)
XLA Modules:
  0.0 38.3 jit_solution(8792396677488254174)
XLA Ops:
  0.0 37.4 %layer.1 = bf16[2,256,1024]{2,1,0:T(8,128)(2,1)S(1)} custom-call(bf16[256,1024]{1,0:T(8,128)(2,1)} %inner.1, bf16[256,4096]{1,0:T(8,128)(2,1)} %proj.1, f32[16,256]{1,0:T(8,128)} %pstep.1, bf16[2,256,1024]{2,1,0:T(8,128)(2,1)} %cin.1, bf16[2,256,1024]{2,1,0:T(8,128)(2,1)} %gate.1, bf16[2,256,4096]{2,1,0:T(8,128)(2,1)} %cproj.1, f32[16,2,256]{2,1,0:T(2,128)} %sstep.1, ...), custom_call_target="tpu_custom_call" | custom-call | tf_op jit(solution)/shard_map/layer/pallas_call | solution.py:732
  37.4 1.0 %copy.14 = bf16[2,256,1024]{2,1,0:T(8,128)(2,1)} copy(bf16[2,256,1024]{2,1,0:T(8,128)(2,1)S(1)} %layer.1) | data formatting | bytes 2097152

commit v5 on v4

--- a/solution.py
+++ b/solution.py
@@ -30,7 +30,7 @@
 
 EDGE = 8
 HALVES = 2
-PIECE = HEAD_WIDTH // HALVES
+PIECES = ((0, 16), (16, 48))
 
 R_SIB, R_HALO, R_TAIL, R_MLOG, R_LOG, R_MID = 0, 3, 5, 7, 15, 23
 R_RED = R_MID + CHIPS * HALVES
@@ -369,9 +369,10 @@
     edge_x = (causal_conv(px[0, :16, :], hx[...], taps_x) * wide[0, :16, :]).astype(BF16)
 
     def mid_copy(i, half):
-        rows = pl.ds(i * HEAD_WIDTH + half * PIECE, PIECE)
+        first, count = PIECES[half]
+        rows = pl.ds(i * HEAD_WIDTH + first, count)
         return remote(
-            st.at[rows, :], mid.at[c // 2, pl.ds(half * PIECE, PIECE), :],
+            st.at[rows, :], mid.at[c // 2, pl.ds(first, count), :],
             S_MID + 2 * i + half, R_MID + 2 * (c // 2) + half, 2 * z + c_core, 8 * k + i,
         )
 
@@ -440,7 +441,7 @@
     shifted = cum - jnp.concatenate(log_step, axis=0)
 
     def red_copy(j, half):
-        rows = pl.ds(half * PIECE, PIECE)
+        rows = pl.ds(*PIECES[half])
         return remote(
             mid.at[j, rows, :], red.at[z, rows, :],
             S_RED + 2 * j + half, R_RED + 2 * z + half, 2 * j + k, c,
@@ -463,7 +464,7 @@
             redlog[z] = midlog[j]
 
     for half in range(HALVES):
-        rows = pl.ds(half * PIECE, PIECE)
+        rows = pl.ds(*PIECES[half])
         for j in range(CHIPS):
             @pl.when(no(both(mid_self, c // 2 == j)))
             def _():
@@ -537,7 +538,8 @@
         later = later + redlog[chip]
 
     def mine(half):
-        return ds(c * HEAD_WIDTH + half * PIECE, PIECE)
+        first, count = PIECES[half]
+        return pl.ds(pl.multiple_of(c * HEAD_WIDTH + first, 16), count)
 
     def ag_copy(step, half):
         return remote(
@@ -546,7 +548,7 @@
         )
 
     for half in range(HALVES):
-        rows = pl.ds(half * PIECE, PIECE)
+        rows = pl.ds(*PIECES[half])
         for chip in range(CHIPS):
             @pl.when(z != chip)
             def _():
@@ -608,7 +610,7 @@
             def _():
                 for half in range(HALVES):
                     arrived(
-                        stf.at[pl.ds(source * HEAD_WIDTH + half * PIECE, PIECE), :],
+                        stf.at[pl.ds(source * HEAD_WIDTH + PIECES[half][0], PIECES[half][1]), :],
                         R_AG + HALVES * source + half,
                     )
 

time: 38.4 us -> 38.3 us (level)
  no operation moved by 1% of the time
where the time goes in v5:
time: 38.3 us; the launch traced here: 38.2 us
  Pallas kernels  37.2 us (97%)
  local copies, waits for them, and re-layouts  0.97 us (3%)
    pallas_call x1, Pallas kernels, local(): layer(*[pltpu.with_memory_space_constraint(array, pltpu.HBM) for array in...  37.2 us
    unnamed x1, local copies, waits for them, and re-layouts  0.97 us

profile of v5, /device:TPU:1, one launch (start us, length us, event | category | flops | bytes accessed | tf_op | source)
XLA Modules:
  0.0 38.2 jit_solution(13738544161158896970)
XLA Ops:
  0.0 37.2 %layer.1 = bf16[2,256,1024]{2,1,0:T(8,128)(2,1)S(1)} custom-call(bf16[256,1024]{1,0:T(8,128)(2,1)} %inner.1, bf16[256,4096]{1,0:T(8,128)(2,1)} %proj.1, f32[16,256]{1,0:T(8,128)} %pstep.1, bf16[2,256,1024]{2,1,0:T(8,128)(2,1)} %cin.1, bf16[2,256,1024]{2,1,0:T(8,128)(2,1)} %gate.1, bf16[2,256,4096]{2,1,0:T(8,128)(2,1)} %cproj.1, f32[16,2,256]{2,1,0:T(2,128)} %sstep.1, ...), custom_call_target="tpu_custom_call" | custom-call | tf_op jit(solution)/shard_map/layer/pallas_call | solution.py:734
  37.2 1.0 %copy.14 = bf16[2,256,1024]{2,1,0:T(8,128)(2,1)} copy(bf16[2,256,1024]{2,1,0:T(8,128)(2,1)S(1)} %layer.1) | data formatting | bytes 2097152
